TPU v7x, 128 devices: a whole 4x4x4 slice. The times are simulated.
128 devices in a mesh: fem: 8 (over y, core), bem: 16 (over z, x).
Axes of the slice: x: 4, y: 4, z: 4, core: 2. Of those that a mesh axis runs over, the one named last changes fastest.
Arguments:
- fem_field: float32 [4, 1048576], P(None, ('fem', 'bem')), may hold values from -6 to 6
- elem_mats: float32 [4, 4, 4194304], P(None, None, ('fem', 'bem')), may hold values from -1.8 to 1.8
- elem_nodes: int32 [4, 4194304], P(None, ('fem', 'bem')), may hold values from 0 to 9215
- trace_count: int32 [128], P(('fem', 'bem')), may hold values from 1 to 16384, 1572864 in all
- trace_node: int32 [2097152], P(('fem', 'bem')), may hold values from 0 to 8191
- trace_block: int32 [2097152, 1], P(('fem', 'bem')), may hold values from 0 to 127; in each aligned block of 16384 rows (0 to 16383, 16384 to 32767, ...) at most 256 rows name the same one
- trace_pos: int32 [2097152], P(('fem', 'bem')), may hold values from 0 to 1151
- trace_weight: float32 [2097152], P(('fem', 'bem')), may hold values from 0.2 to 1
- near_tiles: bfloat16 [16, 72, 128, 128], P('bem', 'fem'), may hold values from -0.5 to 0.5
- left_basis: bfloat16 [16, 16, 32, 9216], P('bem', None, None, 'fem'), may hold values from -0.0625 to 0.0625
- right_basis: bfloat16 [16, 16, 32, 9216], P('bem', None, None, 'fem'), may hold values from -0.375 to 0.375
- bem_field: float32 [16, 4, 9216], P('bem', None, 'fem'), may hold values from -6 to 6
Outputs:
- fem_out: float32 [4, 1048576], P(None, ('fem', 'bem'))
- bem_flux: float32 [16, 4, 9216], P('bem', None, 'fem')
Inputs may be any that keep to these rules, and one draw needn't show every extreme that they name: `trace_block`: among the 16384 rows of one partition no BEM block is named by more than 256 rows, and some block is named by exactly 256 rows. `trace_count`: rows of a partition at or beyond its count are padding; some partition has 16384 live rows.
All inputs are finite; a program needn't handle non-finite values. No bound on the sum of `trace_count` on one device may be relied on, other than what follows from the above.
Results may differ from a plain program's by a relative error of at most 0.0003.
Values sent between devices are 32-bit elements; how exact they have to be, the bound alone decides.
A program may use at most 192 MiB of HBM per device.

v0:
```python
import jax
import jax.numpy as jnp
from jax import lax
from jax.sharding import PartitionSpec as P

REACH = 512
TILE = 128


def with_halo(block, sides, width):
    for axis, dim in sides:
        count = lax.axis_size(axis)
        forward = [(i, i + 1) for i in range(count - 1)]
        backward = [(target, source) for source, target in forward]
        low = lax.ppermute(
            lax.slice_in_dim(block, block.shape[dim] - width, None, axis=dim), axis, forward
        )
        high = lax.ppermute(lax.slice_in_dim(block, 0, width, axis=dim), axis, backward)
        block = jnp.concatenate([low, block, high], axis=dim)
    return block


def stiffness_local(fem_field, elem_mats, elem_nodes):
    rhs_count = fem_field.shape[0]
    node_count = fem_field.shape[1]
    extended = with_halo(fem_field, ((("fem", "bem"), 1),), REACH)
    corner = extended[:, elem_nodes]
    owned_mask = ((elem_nodes >= REACH) & (elem_nodes < REACH + node_count)).astype(jnp.float32)
    target = jnp.where(owned_mask > 0, elem_nodes - REACH, node_count)
    columns = []
    for column_at in range(4):
        summed = elem_mats[0, column_at][None, :] * corner[:, 0]
        for row_at in range(1, 4):
            summed = summed + elem_mats[row_at, column_at][None, :] * corner[:, row_at]
        columns.append(summed * owned_mask[column_at][None, :])
    contrib = jnp.stack(columns, axis=1)
    assembled = jnp.zeros((rhs_count, node_count), jnp.float32)
    return assembled.at[:, target.reshape(-1)].add(contrib.reshape(rhs_count, -1), mode="drop")


def per_device(
    fem_field,
    elem_mats,
    elem_nodes,
    trace_count,
    trace_node,
    trace_block,
    trace_pos,
    trace_weight,
    near_tiles,
    left_basis,
    right_basis,
    bem_field,
):
    rhs_count = fem_field.shape[0]
    stiffness = stiffness_local(fem_field, elem_mats, elem_nodes)
    fem_size = lax.axis_size("fem")
    bem_size = lax.axis_size("bem")
    bucket_count = fem_size * bem_size
    trace_rows = trace_node.shape[0]
    capacity = 2 * trace_rows // bucket_count
    live_rows = jnp.arange(trace_rows, dtype=jnp.int32) < trace_count[0]
    trace_coef = jnp.where(live_rows, trace_weight, jnp.zeros_like(trace_weight))
    values = fem_field[:, trace_node] * trace_coef[None, :]
    block_id = trace_block[:, 0]
    bucket = block_id % fem_size * bem_size + block_id // fem_size
    one_hot = (bucket[:, None] == jnp.arange(bucket_count, dtype=jnp.int32)[None, :]).astype(
        jnp.int32
    )
    position = jnp.sum(jnp.cumsum(one_hot, axis=0) * one_hot, axis=1) - 1
    slot_index = bucket * capacity + position
    send_values = (
        jnp.zeros((rhs_count, bucket_count * capacity), jnp.float32).at[:, slot_index].set(values)
    )
    send_values = send_values.reshape(rhs_count, fem_size, bem_size, capacity)
    send_offsets = (
        jnp.zeros((1, bucket_count * capacity), jnp.float32)
        .at[:, slot_index]
        .set(trace_pos.astype(jnp.float32)[None, :])
    )
    send_offsets = send_offsets.reshape(1, fem_size, bem_size, capacity)
    got_values, got_offsets = (
        lax.all_to_all(
            lax.all_to_all(send_values, "fem", split_axis=1, concat_axis=1, tiled=True),
            "bem",
            split_axis=2,
            concat_axis=2,
            tiled=True,
        ),
        lax.all_to_all(
            lax.all_to_all(send_offsets, "fem", split_axis=1, concat_axis=1, tiled=True),
            "bem",
            split_axis=2,
            concat_axis=2,
            tiled=True,
        ),
    )
    offsets = got_offsets.reshape(-1).astype(jnp.int32)
    sub_size = bem_field.shape[2]
    traces = (
        jnp.zeros((rhs_count, sub_size), jnp.float32)
        .at[:, offsets]
        .add(got_values.reshape(rhs_count, -1))
    )
    coupling_part = jnp.einsum(
        "ckj,rj->crk", left_basis[0].astype(jnp.float32), traces, precision=lax.Precision.HIGHEST
    )
    coupling = lax.psum(coupling_part, "fem")
    near_field = jnp.einsum(
        "tiq,rti->rtq",
        near_tiles[0].astype(jnp.float32),
        traces.reshape(rhs_count, -1, TILE),
        precision=lax.Precision.HIGHEST,
    ).reshape(rhs_count, sub_size)
    own_slice = lax.axis_index("bem")
    far_basis = right_basis[0]
    far_term = jnp.einsum(
        "crk,ckj->crj", coupling, far_basis.astype(jnp.float32), precision=lax.Precision.HIGHEST
    )
    is_own = jnp.arange(lax.axis_size("bem") * 1, dtype=jnp.int32) == own_slice
    summed = lax.psum_scatter(
        far_term + jnp.where(is_own[:, None, None], near_field[None], 0.0),
        "bem",
        scatter_dimension=0,
        tiled=True,
    )
    bem_flux = summed + bem_field
    whole_flux = lax.all_gather(bem_flux, ("fem", "bem"), axis=0, tiled=True)
    picked = whole_flux[bucket, :, trace_pos]
    returned = picked.T * trace_coef[None, :]
    fem_out = stiffness + jnp.zeros_like(stiffness).at[:, trace_node].add(returned)
    return (fem_out, bem_flux)


def solution(mesh):
    placed = (
        P(None, ("fem", "bem")),
        P(None, None, ("fem", "bem")),
        P(None, ("fem", "bem")),
        P(("fem", "bem")),
        P(("fem", "bem")),
        P(("fem", "bem"), None),
        P(("fem", "bem")),
        P(("fem", "bem")),
        P("bem", "fem", None, None),
        P("bem", None, None, "fem"),
        P("bem", None, None, "fem"),
        P("bem", None, "fem"),
    )
    return jax.shard_map(
        per_device,
        mesh=mesh,
        in_specs=placed,
        out_specs=(P(None, ("fem", "bem")), P("bem", None, "fem")),
        check_vma=False,
    )
```

profile of v0, /device:TPU:1, one launch (start us, length us, event | category | flops | bytes accessed | tf_op | source)
XLA Modules:
  0.0 2098.5 jit_solution(3777039990761520627)
XLA Ops:
  7.2 0.8 fusion.40
  8.0 3.9 collective-permute-start
  11.9 7.2 collective-permute-start.1
  19.2 0.9 fusion.41
  20.1 1.5 fusion.31
  21.7 1.0 fusion.6
  22.7 3.2 copy-done.2
  26.3 8.3 broadcast_add_fusion
  34.5 9.3 copy.101
  43.8 8.4 fusion.2
  52.3 60.4 %scatter_custom_fusion.1 = f32[32768]{0:T(1024)S(1)} fusion(s32[16384]{0:T(1024)S(1)} %bitcast.124, f32[16384]{0:T(1024)S(1)} %get-tuple-element.44, f32[]{:T(128)} %constant.22.clone.1), kind=kCustom, calls=%fused_computation.66 | custom fusion | bytes 131076 | tf_op jit(solution)/shard_map/scatter | solution.py:79
  113.4 4.6 all-to-all-start
  118.6 1.1 fusion.39
  120.4 1.3 compare_select_fusion
  121.8 2.8 fusion.38
  126.6 4.1 all-to-all-start.1
  130.7 2.6 copy.104
  133.4 147.3 %scatter_custom_fusion.2 = f32[4,32768]{0,1:T(8,128)} fusion(s32[16384]{0:T(1024)S(1)} %bitcast.125, f32[]{:T(128)} %constant.22.clone.1, f32[16384]{0:T(1024)S(1)} %fusion.34, f32[4,8192]{0,1:T(8,128)} %copy.104, s32[16384]{0:T(1024)S(1)} %get-tuple-element.42), kind=kCustom, calls=%fused_computation.8 | custom fusion | flops 65536 | bytes 786436 | tf_op jit(solution)/shard_map/scatter | solution.py:73
  280.6 10.7 copy.106
  291.9 5.1 all-to-all-start.2
  297.0 2.9 copy.95
  299.9 432.8 %gather_fusion = f32[131072,4]{1,0:T(8,128)} fusion(f32[4,9216]{0,1:T(8,128)} %copy.95, s32[131072]{0:T(1024)S(1)} %broadcast_clamp_fusion), kind=kCustom, calls=%fused_computation | custom fusion | bytes 4718592 | tf_op jit(solution)/shard_map/gather | solution.py:27
  732.7 34.3 %copy.96 = f32[4,32768,4]{1,0,2:T(4,128)S(1)} copy(f32[4,32768,4]{2,1,0:T(8,128)} %bitcast.2) | data formatting | bytes 4194304 | tf_op jit(solution)/shard_map/gather | solution.py:27
  767.0 0.9 convert_element_type.30
  768.0 0.8 copy.120
  768.7 2.2 copy.107
  770.9 7.1 all-to-all-start.3
  778.0 1.7 compare_select_fusion.2
  779.7 9.4 all-to-all-done.3
  789.1 1.3 copy.108
  790.5 1.1 copy.121
  791.6 9.0 copy.109
  800.6 205.3 %scatter_custom_fusion.3 = f32[4,1152]{0,1:T(8,128)} fusion(s32[32768]{0:T(1024)} %bitcast.123, f32[32768,4]{1,0:T(8,128)} %copy.109, f32[]{:T(128)} %constant.22.clone.1), kind=kCustom, calls=%fused_computation.47 | custom fusion | flops 131072 | bytes 18944 | tf_op jit(solution)/shard_map/scatter-add | solution.py:103
  1006.0 5.9 fusion.17
  1011.8 27.9 %psum.7 = f32[16,4,32]{2,1,0:T(4,128)} all-reduce(f32[16,4,32]{2,1,0:T(4,128)} %fusion.17), channel_id=1, replica_groups=mesh['fem'=8,'bem'=16] {'fem'}, use_global_device_ids=true, to_apply=%region_7.8 | all-reduce | flops 2048 | bytes 16384 | tf_op jit(solution)/shard_map/psum | solution.py:108
  1039.7 1.7 convolution_bitcast_fusion
  1041.4 2.1 convolution_add_fusion
  1043.6 4.3 add_multiply_fusion.1
  1047.9 75.3 %all-reduce.3.cloned.1.call-done = f32[16,4,1152]{2,1,0:T(4,128)} async-done(((f32[16,4,1152]{2,1,0:T(4,128)}), f32[16,4,1152]{2,1,0:T(4,128)}) %all-reduce.3.cloned.1.call-update) | async-done | bytes 294928
  1123.2 2.0 dynamic-slice_add_fusion
  1125.2 4.2 add_multiply_fusion.3
  1129.4 1.9 pad_maximum_fusion
  1131.3 30.9 %copy.116 = f32[4,4,32768]{0,2,1:T(8,128)} copy(f32[4,4,32768]{2,1,0:T(4,128)S(1)} %pad_maximum_fusion) | data formatting | bytes 4194304 | tf_op jit(solution)/shard_map/reshape | solution.py:38
  1162.2 696.1 %scatter_custom_fusion = f32[4,8192]{0,1:T(8,128)} fusion(s32[131072]{0:T(1024)} %bitcast.113, f32[131072,4]{1,0:T(8,128)} %bitcast.24, f32[]{:T(128)} %constant.22.clone.1), kind=kCustom, calls=%fused_computation.28 | custom fusion | flops 524288 | bytes 131584 | tf_op jit(solution)/shard_map/scatter-add | solution.py:38
  1858.3 33.9 %copy.112 = f32[128,4,1152]{1,2,0:T(8,128)} copy(f32[128,4,1152]{2,1,0:T(4,128)} %all-gather.2.cloned.1.call-done) | data formatting | bytes 4718592 | tf_op jit(solution)/shard_map/all_gather | solution.py:128
  1892.2 189.9 %scatter_custom_fusion.4 = f32[4,8192]{0,1:T(8,128)} fusion(s32[16384]{0:T(1024)} %get-tuple-element.43, f32[16384]{0:T(1024)S(1)} %fusion.34, f32[]{:T(128)} %constant.22.clone.1, f32[128,4,1152]{1,2,0:T(8,128)} %copy.112, s32[16384]{0:T(1024)S(1)} %bitcast.122), kind=kCustom, calls=%fused_computation.13 | custom fusion | flops 131072 | bytes 75760128 | tf_op jit(solution)/shard_map/scatter-add | solution.py:131
  2082.0 5.9 add.183
  2087.9 3.5 copy.113
  (50 shorter events, 4.7 us)
Async XLA Ops:
  7.2 1034.3 %copy-start = (bf16[1,16,32,1152]{3,2,1,0:T(8,128)(2,1)S(1)}, bf16[1,16,32,1152]{3,2,1,0:T(8,128)(2,1)}, u32[]{:S(2)}) copy-start(bf16[1,16,32,1152]{3,2,1,0:T(8,128)(2,1)} %param.22) | copy-start | bytes 3538948
  8.0 289.0 %collective-permute-start = (f32[4,512]{1,0:T(4,128)S(1)}, f32[4,512]{1,0:T(4,128)S(1)}, u32[]{:S(2)}, u32[]{:S(2)}) collective-permute-start(f32[4,512]{1,0:T(4,128)S(1)} %get-tuple-element.40), channel_id=1, source_target_pairs={{0,1},{1,2},{2,3},{3,4},{4,5},{5,6},{6,7},{7,8},{8,9},{9,10},{10,1... | collective-permute-start | bytes 24584 | tf_op jit(solution)/shard_map/ppermute | solution.py:15
  11.9 285.1 %collective-permute-start.1 = (f32[4,512]{1,0:T(4,128)S(1)}, f32[4,512]{1,0:T(4,128)S(1)}, u32[]{:S(2)}, u32[]{:S(2)}) collective-permute-start(f32[4,512]{1,0:T(4,128)S(1)} %get-tuple-element.41), channel_id=1, source_target_pairs={{1,0},{2,1},{3,2},{4,3},{5,4},{6,5},{7,6},{8,7},{9,8},{10,9},{11,1... | collective-permute-start | bytes 24584 | tf_op jit(solution)/shard_map/ppermute | solution.py:18
  22.7 3.2 copy-start.2
  43.8 74.2 %copy-start.3 = (s32[4,32768]{1,0:T(4,128)S(1)}, s32[4,32768]{1,0:T(4,128)}, u32[]{:S(2)}) copy-start(s32[4,32768]{1,0:T(4,128)} %param.14) | copy-start | bytes 1572868
  52.2 72.4 %copy-start.7 = (s32[16384]{0:T(1024)S(1)}, s32[16384]{0:T(1024)}, u32[]{:S(2)}) copy-start(s32[16384]{0:T(1024)} %param.16) | copy-start | bytes 196612
  52.2 78.5 %copy-start.8 = (f32[16384]{0:T(1024)S(1)}, f32[16384]{0:T(1024)}, u32[]{:S(2)}) copy-start(f32[16384]{0:T(1024)} %param.19) | copy-start | bytes 196612
  52.2 78.5 %copy-start.5 = (f32[4,8192]{1,0:T(4,128)S(1)}, f32[4,8192]{1,0:T(4,128)}, u32[]{:S(2)}) copy-start(f32[4,8192]{1,0:T(4,128)} %param.12) | copy-start | bytes 393220
  113.4 12.4 all-to-all-start
  118.0 3.8 copy-start.4
  126.6 165.4 %all-to-all-start.1 = ((f32[1,8,16,256]{3,1,0,2:T(8,128)}), f32[1,8,16,256]{3,1,0,2:T(8,128)S(1)}, u32[]{:S(2)}, u32[]{:S(2)}) async-start(f32[1,8,16,256]{3,1,0,2:T(8,128)} %copy.102), calls=%async_computation.1 | async-start | bytes 262144 | tf_op jit(solution)/shard_map/all_to_all | solution.py:90
  280.6 10.7 copy-start.9
  291.9 5.1 copy-start.6
  291.9 476.8 %all-to-all-start.2 = ((f32[4,8,16,256]{3,2,0,1:T(8,128)}), f32[4,8,16,256]{3,2,0,1:T(8,128)}, u32[]{:S(2)}, u32[]{:S(2)}) async-start(f32[4,8,16,256]{3,2,0,1:T(8,128)} %copy.106), calls=%async_computation.2 | async-start | bytes 1048576 | tf_op jit(solution)/shard_map/all_to_all | solution.py:84
  770.9 18.2 all-to-all-start.3
  778.0 345.2 %all-reduce.3.cloned.1.call-start = ((), (), s32[]{:S(2)}) async-start(), calls=%async_computation.5 | async-start | bytes 589824
  1043.5 814.8 %all-gather.2.cloned.1.call-start = ((), (), s32[]{:S(2)}) async-start(), calls=%async_computation.4 | async-start | bytes 2377728 | tf_op jit(solution)/shard_map/all_gather | solution.py:128
  1892.2 199.2 %copy-start.1 = (bf16[1,16,32,1152]{3,2,1,0:T(8,128)(2,1)S(1)}, bf16[1,16,32,1152]{3,2,1,0:T(8,128)(2,1)}, u32[]{:S(2)}) copy-start(bf16[1,16,32,1152]{3,2,1,0:T(8,128)(2,1)} %param.22) | copy-start | bytes 3538948
Sparse Core Ops, SparseCore 0:
  1043.7 79.4 all-reduce.2
  1126.7 65.6 all-gather.1
where the time goes:
time: 2110 us; the launch traced here: 2100 us
  other arithmetic  1280 us (61%)
  local copies, waits for them, and re-layouts  646 us (31%)
  waiting for transfers between devices  84.8 us (4%)
  starting transfers between devices  32.1 us (2%)
  blocking collectives  27.9 us (1%)
    scatter-add x1, other arithmetic, stiffness_local(): assembled.at[:, target.reshape(-1)]  696 us
    gather x2, local copies, waits for them, and re-layouts, stiffness_local(): corner = extended[:, elem_nodes]  467 us
    scatter-add x1, other arithmetic, per_device(): traces = jnp.zeros((rhs_count, sub_size), jnp.float32).at[:, offsets].add...  205 us
    scatter-add x1, other arithmetic, per_device(): jnp.zeros_like(stiffness).at[:, trace_node].add(returned)  190 us
    scatter x1, other arithmetic, per_device(): jnp.zeros((rhs_count, bucket_count * capacity), jnp.float32)  147 us
    unnamed x3, waiting for transfers between devices  75.3 us
    scatter x1, local copies, waits for them, and re-layouts, per_device(): send_offsets = jnp.zeros((1, bucket_count * capacity), jnp.float32).at[:,...  60.4 us
  transfers between devices with their start and end apart: 8, of which 2 were waited for; matrix products, arithmetic and copies ran while one was open for 70% of the time, Pallas kernels for 0%

commit v1 on v0

v1 whole, which is shorter than its diff:
```python
import functools

import jax
import jax.numpy as jnp
from jax import lax
from jax.experimental import pallas as pl
from jax.experimental.pallas import tpu as pltpu
from jax.sharding import PartitionSpec as P

REACH = 512
bf16 = jnp.bfloat16
f32 = jnp.float32
i32 = jnp.int32
MESH = pl.DeviceIdType.MESH
NT = (((1,), (1,)), ((), ()))
VMEM_LIMIT = 48 << 20


def iota(shape, dim):
    return lax.broadcasted_iota(i32, shape, dim)


def to_bf(x):
    return x.astype(f32).astype(bf16)


def onehot(rows, index):
    shape = (rows, index.shape[1])
    return jnp.where(
        to_bf(iota(shape, 0)) == jnp.broadcast_to(index, shape),
        jnp.ones((), bf16),
        jnp.zeros((), bf16),
    )


def split8(x):
    hi = x.astype(bf16).astype(f32)
    return jnp.where(iota(x.shape, 0) < 4, hi, x - hi)


def split_table(t):
    hi = t.astype(bf16)
    return jnp.concatenate([hi, (t - hi.astype(f32)).astype(bf16)], 1)


def pick(table, hot, q, groups):
    r = jnp.dot(table, jnp.concatenate([hot, hot], 0), preferred_element_type=f32)
    shape = (8, hot.shape[1])
    qh = jnp.broadcast_to(q, shape) - jnp.where(iota(shape, 0) >= 4, 1, 0)
    acc = jnp.where(qh == 0, r[0:8], 0.0)
    for j in range(1, groups):
        acc = jnp.where(qh == 2 * j, r[8 * j : 8 * j + 8], acc)
    return acc + pltpu.roll(acc, 4, axis=0)


def spread(part, q, groups):
    part = part.astype(bf16)
    p16 = jnp.concatenate([part, part], 0)
    qv = to_bf(jnp.broadcast_to(q, p16.shape) - jnp.where(iota(p16.shape, 0) >= 8, 1, 0))
    zero = jnp.zeros((), bf16)
    return jnp.concatenate(
        [jnp.where(qv == jnp.asarray(2 * j, bf16), p16, zero) for j in range(groups)], 0
    )


def first_step():
    return pl.program_id(0) == 0


def elem_kernel(t_ref, mats_ref, nodes_ref, out_ref, table):
    @pl.when(first_step())
    def _():
        out_ref[...] = jnp.zeros_like(out_ref)
        table[...] = split_table(t_ref[...])

    nodes = nodes_ref[...]
    hots, xs = [], []
    for a in range(4):
        n = nodes[a : a + 1]
        hot = onehot(256, to_bf(n & 255))
        hots.append(hot)
        xs.append(pick(table[...], hot, n >> 8, 18))
    total = None
    for b in range(4):
        c = mats_ref[pl.ds(b, 1), :] * xs[0]
        for a in range(1, 4):
            c = c + mats_ref[pl.ds(4 * a + b, 1), :] * xs[a]
        d = lax.dot_general(
            spread(split8(c), (nodes[b : b + 1] >> 8) - 2, 16),
            hots[b],
            NT,
            preferred_element_type=f32,
        )
        total = d if total is None else total + d
    out_ref[...] += total


def elem_call(table, mats, nodes):
    count = nodes.shape[1]
    eb = 512
    return pl.pallas_call(
        elem_kernel,
        grid=(count // eb,),
        in_specs=[
            pl.BlockSpec((144, 256), lambda i: (0, 0)),
            pl.BlockSpec((16, eb), lambda i: (0, i)),
            pl.BlockSpec((4, eb), lambda i: (0, i)),
        ],
        out_specs=pl.BlockSpec((256, 256), lambda i: (0, 0)),
        out_shape=jax.ShapeDtypeStruct((256, 256), f32),
        scratch_shapes=[pltpu.VMEM((144, 512), bf16)],
        compiler_params=pltpu.CompilerParams(vmem_limit_bytes=VMEM_LIMIT),
        name="elements",
    )(table, mats, nodes)


def bucket_kernel(
    count_ref, t_ref, node_ref, block_ref, pos_ref, weight_ref, out_ref, table, acc, carry
):
    step = pl.program_id(0)
    rb = node_ref.shape[1]

    @pl.when(step == 0)
    def _():
        acc[...] = jnp.zeros_like(acc)
        carry[...] = jnp.zeros_like(carry)
        table[...] = split_table(t_ref[...])

    node, pos, block = node_ref[...], pos_ref[...], block_ref[...]
    row = step * rb + iota((1, rb), 1)
    coef = jnp.where(row < count_ref[0], weight_ref[...], 0.0)
    bucket = to_bf((block & 7) * 16 + (block >> 3))

    owner = onehot(128, bucket)
    upper = jnp.where(iota((rb, rb), 0) <= iota((rb, rb), 1), 1.0, 0.0).astype(bf16)
    counts = jnp.dot(owner, upper, preferred_element_type=f32)
    before = carry[:, 0:1]
    rank = jnp.sum(owner.astype(f32) * (counts + before), axis=0, keepdims=True) - 1.0
    carry[...] = jnp.broadcast_to(before + counts[:, rb - 1 : rb], carry.shape)
    slot = onehot(256, rank.astype(bf16))

    x = pick(table[...], onehot(256, to_bf(node & 255)), node >> 8, 16)
    vals = split8(x * coef)
    hi = coef.astype(bf16).astype(f32)
    sub = iota((8, rb), 0)
    rest = jnp.zeros((8, rb), f32)
    highs = (pos >> 7).astype(f32), (node >> 8).astype(f32), hi
    lows = (pos & 127).astype(f32), (node & 255).astype(f32), coef - hi
    for i in range(3):
        rest = jnp.where(sub == i, jnp.broadcast_to(highs[i], (8, rb)), rest)
        rest = jnp.where(sub == i + 4, jnp.broadcast_to(lows[i], (8, rb)), rest)
    p16 = jnp.concatenate([vals.astype(bf16), rest.astype(bf16)], 0)
    b16 = jnp.broadcast_to(bucket, p16.shape)
    zero = jnp.zeros((), bf16)
    m2 = jnp.concatenate(
        [jnp.where(b16 == jnp.asarray(b, bf16), p16, zero) for b in range(128)], 0
    )
    acc[...] += lax.dot_general(m2, slot, NT, preferred_element_type=f32)

    @pl.when(step == pl.num_programs(0) - 1)
    def _():
        @pl.loop(0, 128)
        def _(b):
            at = pl.multiple_of(b * 16, 16)
            a = acc[pl.ds(at, 8), :]
            c = acc[pl.ds(at + 8, 8), :]
            s = iota(c.shape, 0)
            c = c * jnp.where(s == 0, 128.0, jnp.where(s == 1, 256.0, 1.0))
            out_ref[b] = jnp.where(s < 4, a + pltpu.roll(a, 4, axis=0), c + pltpu.roll(c, 4, axis=0))


def bucket_call(count, table, node, block, pos, weight):
    rows = node.shape[1]
    rb = 512
    row_spec = pl.BlockSpec((1, rb), lambda i: (0, i))
    return pl.pallas_call(
        bucket_kernel,
        grid=(rows // rb,),
        in_specs=[
            pl.BlockSpec(memory_space=pltpu.SMEM),
            pl.BlockSpec((128, 256), lambda i: (0, 0)),
            row_spec,
            row_spec,
            row_spec,
            row_spec,
        ],
        out_specs=pl.BlockSpec((128, 8, 256), lambda i: (0, 0, 0)),
        out_shape=jax.ShapeDtypeStruct((128, 8, 256), f32),
        scratch_shapes=[
            pltpu.VMEM((128, 512), bf16),
            pltpu.VMEM((2048, 256), f32),
            pltpu.VMEM((128, 128), f32),
        ],
        compiler_params=pltpu.CompilerParams(vmem_limit_bytes=VMEM_LIMIT),
        name="buckets",
    )(count, table, node, block, pos, weight)


def exchange_kernel(src, dst, send_sem, recv_sem, local_sem):
    count = 128
    wide = lax.axis_size("bem")
    me = lax.axis_index("fem") * wide + lax.axis_index("bem")
    barrier = pltpu.get_barrier_semaphore()

    @pl.loop(1, count)
    def _(k):
        peer = lax.rem(me + k, count)
        pl.semaphore_signal(
            barrier, inc=1, device_id=(peer // wide, lax.rem(peer, wide)), device_id_type=MESH
        )

    own = pltpu.make_async_copy(src.at[me], dst.at[me], local_sem)
    own.start()
    pl.semaphore_wait(barrier, count - 1)

    @pl.loop(1, count)
    def _(k):
        peer = lax.rem(me + k, count)
        pltpu.make_async_remote_copy(
            src_ref=src.at[peer],
            dst_ref=dst.at[me],
            send_sem=send_sem,
            recv_sem=recv_sem,
            device_id=(peer // wide, lax.rem(peer, wide)),
            device_id_type=MESH,
        ).start()

    own.wait()
    most = pl.ds(0, count - 1)
    pltpu.make_async_copy(src.at[most], src.at[most], send_sem).wait()
    pltpu.make_async_copy(dst.at[most], dst.at[most], recv_sem).wait()


def exchange_call(parts, collective_id, name):
    return pl.pallas_call(
        exchange_kernel,
        in_specs=[pl.BlockSpec(memory_space=pltpu.VMEM)],
        out_specs=pl.BlockSpec(memory_space=pltpu.VMEM),
        out_shape=jax.ShapeDtypeStruct(parts.shape, f32),
        scratch_shapes=[pltpu.SemaphoreType.DMA] * 3,
        compiler_params=pltpu.CompilerParams(
            collective_id=collective_id, has_side_effects=True, vmem_limit_bytes=VMEM_LIMIT
        ),
        name=name,
    )(parts)


def owner_kernel(got_ref, left_ref, near_ref, coupling_ref, near_out_ref, acc):
    step = pl.program_id(0)

    @pl.when(step == 0)
    def _():
        acc[...] = jnp.zeros_like(acc)

    tile = jnp.concatenate([got_ref[s] for s in range(got_ref.shape[0])], 1)
    vals = jnp.where(iota(tile.shape, 0) < 4, tile, pltpu.roll(tile, 4, axis=0))
    pos = tile[4:5].astype(i32)
    acc[...] += lax.dot_general(
        spread(split8(vals), pos >> 7, 5),
        onehot(128, to_bf(pos & 127)),
        NT,
        preferred_element_type=f32,
    )

    @pl.when(step == pl.num_programs(0) - 1)
    def _():
        parts = []
        for t in range(9):
            a = acc[8 * t : 8 * t + 8]
            part = split8(a + pltpu.roll(a, 4, axis=0)).astype(bf16)
            parts.append(part)
            n = jnp.dot(part, near_ref[t], preferred_element_type=f32)
            near_out_ref[:, 128 * t : 128 * t + 128] = (n + pltpu.roll(n, 4, axis=0))[0:4]
        c = lax.dot_general(
            jnp.concatenate(parts, 1), left_ref[...], NT, preferred_element_type=f32
        )
        coupling_ref[...] = (c + pltpu.roll(c, 4, axis=0))[0:4]


def owner_call(got, left, near):
    sb = 4
    return pl.pallas_call(
        owner_kernel,
        grid=(128 // sb,),
        in_specs=[
            pl.BlockSpec((sb, 8, 256), lambda i: (i, 0, 0)),
            pl.BlockSpec((512, 1152), lambda i: (0, 0)),
            pl.BlockSpec((9, 128, 128), lambda i: (0, 0, 0)),
        ],
        out_specs=[
            pl.BlockSpec((4, 512), lambda i: (0, 0)),
            pl.BlockSpec((4, 1152), lambda i: (0, 0)),
        ],
        out_shape=[jax.ShapeDtypeStruct((4, 512), f32), jax.ShapeDtypeStruct((4, 1152), f32)],
        scratch_shapes=[pltpu.VMEM((80, 128), f32)],
        compiler_params=pltpu.CompilerParams(vmem_limit_bytes=VMEM_LIMIT),
        name="owner",
    )(got, left, near)


def flux_kernel(
    part_ref, near_ref, right_ref, field_ref, out_ref, parts, shares, sums, sems, local_sem
):
    fems, bems = 8, 16
    f, b = lax.axis_index("fem"), lax.axis_index("bem")
    barrier = pltpu.get_barrier_semaphore()
    for k in range(1, fems):
        pl.semaphore_signal(
            barrier, inc=1, device_id=(lax.rem(f + k, fems), b), device_id_type=MESH
        )
    for k in range(1, bems):
        pl.semaphore_signal(
            barrier, inc=1, device_id=(f, lax.rem(b + k, bems)), device_id_type=MESH
        )
    pl.semaphore_wait(barrier, fems + bems - 2)

    for k in range(1, fems):
        pltpu.make_async_remote_copy(
            src_ref=part_ref,
            dst_ref=parts.at[f],
            send_sem=sems.at[0],
            recv_sem=sems.at[1],
            device_id=(lax.rem(f + k, fems), b),
            device_id_type=MESH,
        ).start()
    own = pltpu.make_async_copy(part_ref, parts.at[f], local_sem)
    own.start()
    own.wait()
    most = parts.at[pl.ds(0, fems - 1)]
    pltpu.make_async_copy(most, most, sems.at[0]).wait()
    pltpu.make_async_copy(most, most, sems.at[1]).wait()

    total = parts[0]
    for k in range(1, fems):
        total = total + parts[k]
    for half in range(2):
        c = total[:, 256 * half : 256 * half + 256]
        c = split8(jnp.concatenate([c, c], 0))
        stacked = jnp.concatenate([c] * 8, 0)
        shape = stacked.shape
        diag = jnp.where((iota(shape, 0) >> 3) == (iota(shape, 1) >> 5), stacked, 0.0).astype(bf16)
        far = jnp.dot(
            diag, right_ref[256 * half : 256 * half + 256], preferred_element_type=f32
        )
        for s in range(8):
            a = far[8 * s : 8 * s + 8]
            shares[8 * half + s] = (a + pltpu.roll(a, 4, axis=0))[0:4]
    shares[b] = shares[b] + near_ref[...]

    for k in range(1, bems):
        peer = lax.rem(b + k, bems)
        pltpu.make_async_remote_copy(
            src_ref=shares.at[peer],
            dst_ref=sums.at[b],
            send_sem=sems.at[2],
            recv_sem=sems.at[3],
            device_id=(f, peer),
            device_id_type=MESH,
        ).start()
    own = pltpu.make_async_copy(shares.at[b], sums.at[b], local_sem)
    own.start()
    own.wait()
    most = sums.at[pl.ds(0, bems - 1)]
    pltpu.make_async_copy(most, most, sems.at[2]).wait()
    pltpu.make_async_copy(most, most, sems.at[3]).wait()
    flux = field_ref[...]
    for k in range(bems):
        flux = flux + sums[k]
    out_ref[...] = flux


def flux_call(part, near, right, field):
    vmem = pl.BlockSpec(memory_space=pltpu.VMEM)
    return pl.pallas_call(
        flux_kernel,
        in_specs=[vmem] * 4,
        out_specs=vmem,
        out_shape=jax.ShapeDtypeStruct((4, 1152), f32),
        scratch_shapes=[
            pltpu.VMEM((8, 4, 512), f32),
            pltpu.VMEM((16, 4, 1152), f32),
            pltpu.VMEM((16, 4, 1152), f32),
            pltpu.SemaphoreType.DMA((4,)),
            pltpu.SemaphoreType.DMA,
        ],
        compiler_params=pltpu.CompilerParams(
            collective_id=1, has_side_effects=True, vmem_limit_bytes=VMEM_LIMIT
        ),
        name="flux",
    )(part, near, right, field)


def return_kernel(t_ref, got_ref, out_ref, table):
    @pl.when(first_step())
    def _():
        table[...] = split_table(t_ref[...])

    count = got_ref.shape[0]
    pos = jnp.concatenate([got_ref[s, 4:5] for s in range(count)], 1).astype(i32)
    x = pick(table[...], onehot(128, to_bf(pos & 127)), pos >> 7, 5)
    for s in range(count):
        out_ref[s] = x[0:4, 256 * s : 256 * s + 256]


def return_call(table, got):
    sb = 4
    return pl.pallas_call(
        return_kernel,
        grid=(128 // sb,),
        in_specs=[
            pl.BlockSpec((40, 128), lambda i: (0, 0)),
            pl.BlockSpec((sb, 8, 256), lambda i: (i, 0, 0)),
        ],
        out_specs=pl.BlockSpec((sb, 4, 256), lambda i: (i, 0, 0)),
        out_shape=jax.ShapeDtypeStruct((128, 4, 256), f32),
        scratch_shapes=[pltpu.VMEM((40, 256), bf16)],
        compiler_params=pltpu.CompilerParams(vmem_limit_bytes=VMEM_LIMIT),
        name="returns",
    )(table, got)


def nodes_kernel(stiff_ref, flux_ref, slots_ref, out_ref):
    @pl.when(first_step())
    def _():
        out_ref[...] = stiff_ref[...]

    count = flux_ref.shape[0]
    slots = jnp.concatenate([slots_ref[s] for s in range(count)], 1)
    x = jnp.concatenate([flux_ref[s] for s in range(count)], 1)
    coef = slots[6:7]
    node = slots[5:6].astype(i32)
    x = jnp.concatenate([x, x], 0) * coef
    out_ref[...] += lax.dot_general(
        spread(split8(x), node >> 8, 16),
        onehot(256, to_bf(node & 255)),
        NT,
        preferred_element_type=f32,
    )


def nodes_call(stiff, flux, slots):
    sb = 4
    return pl.pallas_call(
        nodes_kernel,
        grid=(128 // sb,),
        in_specs=[
            pl.BlockSpec((256, 256), lambda i: (0, 0)),
            pl.BlockSpec((sb, 4, 256), lambda i: (i, 0, 0)),
            pl.BlockSpec((sb, 8, 256), lambda i: (i, 0, 0)),
        ],
        out_specs=pl.BlockSpec((256, 256), lambda i: (0, 0)),
        out_shape=jax.ShapeDtypeStruct((256, 256), f32),
        compiler_params=pltpu.CompilerParams(vmem_limit_bytes=VMEM_LIMIT),
        name="nodes",
    )(stiff, flux, slots)


def tiles(x, width):
    return x.reshape(4, -1, width).transpose(1, 0, 2).reshape(-1, width)


def per_device(
    fem_field,
    elem_mats,
    elem_nodes,
    trace_count,
    trace_node,
    trace_block,
    trace_pos,
    trace_weight,
    near_tiles,
    left_basis,
    right_basis,
    bem_field,
):
    both = ("fem", "bem")
    size = lax.axis_size(both)
    ahead = [(i, i + 1) for i in range(size - 1)]
    back = [(i + 1, i) for i in range(size - 1)]
    low = lax.ppermute(fem_field[:, -REACH:], both, ahead)
    high = lax.ppermute(fem_field[:, :REACH], both, back)
    own_table = tiles(fem_field, 256)
    table = jnp.concatenate([tiles(low, 256), own_table, tiles(high, 256)], 0)

    slots = bucket_call(
        trace_count,
        own_table,
        trace_node.reshape(1, -1),
        trace_block.reshape(1, -1),
        trace_pos.reshape(1, -1),
        trace_weight.reshape(1, -1),
    )
    got = exchange_call(slots, 0, "rows_out")
    stiff = elem_call(table, elem_mats.reshape(16, -1), elem_nodes)
    part, near = owner_call(got, left_basis.reshape(512, 1152), near_tiles[0])
    flux = flux_call(part, near, right_basis.reshape(512, 1152), bem_field[0])
    flux_table = jnp.concatenate([tiles(flux, 128), jnp.zeros((4, 128), f32)], 0)
    returned = exchange_call(return_call(flux_table, got), 2, "flux_back")
    out = nodes_call(stiff, returned, slots)
    out = out.reshape(32, 2, 4, 256).sum(1).transpose(1, 0, 2).reshape(4, -1)
    return out, flux[None]


def solution(mesh):
    placed = (
        P(None, ("fem", "bem")),
        P(None, None, ("fem", "bem")),
        P(None, ("fem", "bem")),
        P(("fem", "bem")),
        P(("fem", "bem")),
        P(("fem", "bem"), None),
        P(("fem", "bem")),
        P(("fem", "bem")),
        P("bem", "fem", None, None),
        P("bem", None, None, "fem"),
        P("bem", None, None, "fem"),
        P("bem", None, "fem"),
    )
    return jax.shard_map(
        per_device,
        mesh=mesh,
        in_specs=placed,
        out_specs=(P(None, ("fem", "bem")), P("bem", None, "fem")),
        check_vma=False,
    )
```

time: 2110 us -> 197 us (0.09)
  other arithmetic: 1280 us -> 0.74 us
  local copies, waits for them, and re-layouts: 646 us -> 7.09 us
  Pallas kernels: 0 us -> 176 us
  waiting for transfers between devices: 84.8 us -> 0.01 us
  blocking collectives: 27.9 us -> 0 us
    scatter-add x3 -> x0, other arithmetic: 1090 us -> none  [the longest x1 696 us: stiffness_local(): assembled.at[:, target.reshape(-1)]]
    gather x2 -> x0, local copies, waits for them, and re-layouts: 467 us -> none  [stiffness_local(): corner = extended[:, elem_nodes]]
    pallas_call x0 -> x8, Pallas kernels: none -> 176 us  [the longest x1 61.5 us: elem_call(): pl.pallas_call(elem_kernel, grid=(count // eb,), in_specs=[pl.BlockSpec((...]
    scatter x1 -> x0, other arithmetic: 147 us -> none  [per_device(): jnp.zeros((rhs_count, bucket_count * capacity), jnp.float32)]
    unnamed x3 -> x0, waiting for transfers between devices: 75.3 us -> none
    scatter x1 -> x0, local copies, waits for them, and re-layouts: 60.4 us -> none  [per_device(): send_offsets = jnp.zeros((1, bucket_count * capacity), jnp.float32).at[:,...]
    reshape x4 -> x7, local copies, waits for them, and re-layouts: 51.3 us -> 4.1 us  [the longest x1 3.03 us: per_device(): stiff = elem_call(table, elem_mats.reshape(16, -1), elem_nodes)]
    all_gather x1 -> x0, local copies, waits for them, and re-layouts: 33.9 us -> none  [per_device(): whole_flux = lax.all_gather(bem_flux, ('fem', 'bem'), axis=0, tiled=True)]
  transfers between devices with their start and end apart: 8 -> 2, of which waited for: 2 -> 0; matrix products, arithmetic and copies ran while one was open for 70% -> 2% of each run, Pallas kernels for 0% -> 52%
where the time goes in v1:
time: 197 us
  Pallas kernels  176 us (89%)
  starting transfers between devices  11.2 us (6%)
  local copies, waits for them, and re-layouts  7.09 us (4%)
    pallas_call x1, Pallas kernels, elem_call(): pl.pallas_call(elem_kernel, grid=(count // eb,), in_specs=[pl.BlockSpec((...  61.5 us
    pallas_call x2, Pallas kernels, exchange_call(): pl.pallas_call(exchange_kernel, in_specs=[pl.BlockSpec(memory_space=pltpu...  41.3 us
    pallas_call x1, Pallas kernels, bucket_call(): pl.pallas_call(bucket_kernel, grid=(rows // rb,), in_specs=[pl.BlockSpec(...  33.6 us
    pallas_call x1, Pallas kernels, flux_call(): pl.pallas_call(flux_kernel, in_specs=[vmem] * 4, out_specs=vmem, out_shap...  13.4 us
    pallas_call x1, Pallas kernels, nodes_call(): pl.pallas_call(nodes_kernel, grid=(128 // sb,), in_specs=[pl.BlockSpec((2...  11.4 us
    ppermute x1, starting transfers between devices, per_device(): high = lax.ppermute(fem_field[:, :REACH], both, back)  9.24 us
    pallas_call x1, Pallas kernels, owner_call(): pl.pallas_call(owner_kernel, grid=(128 // sb,), in_specs=[pl.BlockSpec((s...  7.83 us
    pallas_call x1, Pallas kernels, return_call(): pl.pallas_call(return_kernel, grid=(128 // sb,), in_specs=[pl.BlockSpec((...  7.09 us
  transfers between devices with their start and end apart: 2, of which 0 were waited for; matrix products, arithmetic and copies ran while one was open for 2% of the time, Pallas kernels for 52%

profile of v1, /device:TPU:1, one launch (start us, length us, event | category | flops | bytes accessed | tf_op | source)
XLA Modules:
  0.0 196.7 jit_solution(5502179533529921397)
XLA Ops:
  0.6 0.7 fusion
  1.3 9.2 %collective-permute-start.1 = (f32[4,512]{1,0:T(4,128)S(1)}, f32[4,512]{1,0:T(4,128)S(1)}, u32[]{:S(2)}, u32[]{:S(2)}) collective-permute-start(f32[4,512]{1,0:T(4,128)S(1)} %get-tuple-element.7), channel_id=1, source_target_pairs={{1,0},{2,1},{3,2},{4,3},{5,4},{6,5},{7,6},{8,7},{9,8},{10,9},{11,1... | collective-permute-start | bytes 24584 | tf_op jit(solution)/shard_map/ppermute | solution.py:481
  10.6 1.9 collective-permute-start
  12.5 1.0 reshape.58.t_ref
  13.5 0.0 copy-start.5
  13.5 0.0 copy-start.6
  13.5 0.0 copy-start.7
  13.5 0.0 copy-start.8
  13.5 3.0 %reshape.61.mats_ref = f32[16,32768]{1,0:T(8,128)} reshape(f32[4,4,32768]{2,1,0:T(4,128)} %param.13) | data formatting | bytes 4194304 | tf_op jit(solution)/shard_map/reshape | solution.py:494
  16.6 0.0 copy-start.1
  16.6 0.0 copy-start.4
  17.3 0.0 copy-done.5
  17.3 0.0 copy-done.6
  17.3 0.0 copy-done.7
  17.4 0.0 copy-done.8
  17.4 33.6 %buckets.1.src.slots_ref = f32[128,8,256]{2,1,0:T(8,128)S(1)} custom-call(s32[1]{0:T(128)S(6)} %copy.27.count_ref, f32[128,256]{1,0:T(8,128)S(1)} %reshape.58.t_ref, s32[1,16384]{1,0:T(1,128)S(1)} %bitcast.26, s32[1,16384]{1,0:T(1,128)S(1)} %bitcast.27, s32[1,16384]{1,0:T(1,128)S(1)} %bitcast.28, f32[1,16384]{1,0:T(1,128)S(1)} %bitcast.29), custom_call_target="tpu_custom_call" | custom-call | tf_op jit(solution)/shard_map/buckets/pallas_call | solution.py:176
  51.0 0.0 copy-start.2
  51.0 0.0 copy-start.9
  51.0 24.1 %rows_out.1.got_ref = f32[128,8,256]{2,1,0:T(8,128)S(1)} custom-call(f32[128,8,256]{2,1,0:T(8,128)S(1)} %buckets.1.src.slots_ref), custom_call_target="tpu_custom_call" | custom-call | tf_op jit(solution)/shard_map/rows_out/pallas_call | solution.py:235
  75.2 0.0 copy-done.1
  75.2 0.0 copy-done.4
  75.2 7.8 %owner.1 = (f32[4,512]{1,0:T(4,128)S(1)}, f32[4,1152]{1,0:T(4,128)S(1)}) custom-call(f32[128,8,256]{2,1,0:T(8,128)S(1)} %rows_out.1.got_ref, bf16[512,1152]{1,0:T(8,128)(2,1)S(1)} %bitcast.22, bf16[9,128,128]{2,1,0:T(8,128)(2,1)S(1)} %bitcast.24), custom_call_target="tpu_custom_call" | custom-call | tf_op jit(solution)/shard_map/owner/pallas_call | solution.py:282
  83.0 0.0 copy-done.2
  83.0 0.0 copy-done.9
  83.0 0.0 copy-start.3
  83.0 13.4 %flux.1 = f32[4,1152]{1,0:T(4,128)S(1)} custom-call(f32[4,512]{1,0:T(4,128)S(1)} %get-tuple-element.4.part_ref, f32[4,1152]{1,0:T(4,128)S(1)} %get-tuple-element.5.near_ref, bf16[512,1152]{1,0:T(8,128)(2,1)S(1)} %bitcast.23, f32[4,1152]{1,0:T(4,128)S(1)} %bitcast.30), custom_call_target="tpu_custom_call" | custom-call | tf_op jit(solution)/shard_map/flux/pallas_call | solution.py:374
  96.5 7.1 %returns.1.src = f32[128,4,256]{2,1,0:T(4,128)S(1)} custom-call(f32[40,128]{1,0:T(8,128)S(1)} %concatenate.7.t_ref, f32[128,8,256]{2,1,0:T(8,128)S(1)} %rows_out.1.got_ref), custom_call_target="tpu_custom_call" | custom-call | tf_op jit(solution)/shard_map/returns/pallas_call | solution.py:407
  103.6 17.1 %flux_back.1.flux_ref = f32[128,4,256]{2,1,0:T(4,128)S(1)} custom-call(f32[128,4,256]{2,1,0:T(4,128)S(1)} %returns.1.src), custom_call_target="tpu_custom_call" | custom-call | tf_op jit(solution)/shard_map/flux_back/pallas_call | solution.py:235
  120.8 0.0 collective-permute-done.1
  120.8 0.0 collective-permute-done
  120.9 0.0 copy-done.3
  120.9 0.0 copy-start
  120.9 1.6 copy-done
  122.5 61.5 %elements.1.stiff_ref = f32[256,256]{1,0:T(8,128)S(1)} custom-call(f32[144,256]{1,0:T(8,128)S(1)} %pad_maximum_fusion.t_ref, f32[16,32768]{1,0:T(8,128)S(1)} %copy-done, s32[4,32768]{1,0:T(4,128)S(1)} %copy-done.3), custom_call_target="tpu_custom_call" | custom-call | tf_op jit(solution)/shard_map/elements/pallas_call | solution.py:101
  184.0 11.4 %nodes.1 = f32[256,256]{1,0:T(8,128)S(1)} custom-call(f32[256,256]{1,0:T(8,128)S(1)} %elements.1.stiff_ref, f32[128,4,256]{2,1,0:T(4,128)S(1)} %flux_back.1.flux_ref, f32[128,8,256]{2,1,0:T(8,128)S(1)} %buckets.1.src.slots_ref), custom_call_target="tpu_custom_call" | custom-call | tf_op jit(solution)/shard_map/nodes/pallas_call | solution.py:443
  195.3 0.1 reshape.70
  195.4 0.7 reduce_sum.9
  196.1 0.6 copy.28
  (7 shorter events, 0.1 us)
Async XLA Ops:
  1.3 119.5 %collective-permute-start.1 = (f32[4,512]{1,0:T(4,128)S(1)}, f32[4,512]{1,0:T(4,128)S(1)}, u32[]{:S(2)}, u32[]{:S(2)}) collective-permute-start(f32[4,512]{1,0:T(4,128)S(1)} %get-tuple-element.7), channel_id=1, source_target_pairs={{1,0},{2,1},{3,2},{4,3},{5,4},{6,5},{7,6},{8,7},{9,8},{10,9},{11,1... | collective-permute-start | bytes 24584 | tf_op jit(solution)/shard_map/ppermute | solution.py:481
  10.6 110.2 %collective-permute-start = (f32[4,512]{1,0:T(4,128)S(1)}, f32[4,512]{1,0:T(4,128)S(1)}, u32[]{:S(2)}, u32[]{:S(2)}) collective-permute-start(f32[4,512]{1,0:T(4,128)S(1)} %get-tuple-element.6), channel_id=1, source_target_pairs={{0,1},{1,2},{2,3},{3,4},{4,5},{5,6},{6,7},{7,8},{8,9},{9,10},{10,1... | collective-permute-start | bytes 24584 | tf_op jit(solution)/shard_map/ppermute | solution.py:480
  13.5 3.9 %copy-start.5 = (s32[16384]{0:T(1024)S(1)}, s32[16384]{0:T(1024)}, u32[]{:S(2)}) copy-start(s32[16384]{0:T(1024)} %param.16) | copy-start | bytes 196612
  13.5 3.8 %copy-start.6 = (s32[16384,1]{0,1:T(1,128)S(1)}, s32[16384,1]{0,1:T(1,128)}, u32[]{:S(2)}) copy-start(s32[16384,1]{0,1:T(1,128)} %param.17) | copy-start | bytes 196612
  13.5 3.8 %copy-start.7 = (s32[16384]{0:T(1024)S(1)}, s32[16384]{0:T(1024)}, u32[]{:S(2)}) copy-start(s32[16384]{0:T(1024)} %param.18) | copy-start | bytes 196612
  13.5 3.8 %copy-start.8 = (f32[16384]{0:T(1024)S(1)}, f32[16384]{0:T(1024)}, u32[]{:S(2)}) copy-start(f32[16384]{0:T(1024)} %param.19) | copy-start | bytes 196612
  16.6 58.6 %copy-start.1 = (bf16[1,16,32,1152]{3,2,1,0:T(8,128)(2,1)S(1)}, bf16[1,16,32,1152]{3,2,1,0:T(8,128)(2,1)}, u32[]{:S(2)}) copy-start(bf16[1,16,32,1152]{3,2,1,0:T(8,128)(2,1)} %param.21) | copy-start | bytes 3538948
  16.6 58.6 %copy-start.4 = (bf16[1,9,128,128]{3,2,1,0:T(8,128)(2,1)S(1)}, bf16[1,9,128,128]{3,2,1,0:T(8,128)(2,1)}, u32[]{:S(2)}) copy-start(bf16[1,9,128,128]{3,2,1,0:T(8,128)(2,1)} %param.20) | copy-start | bytes 884740
  51.0 32.0 %copy-start.2 = (bf16[1,16,32,1152]{3,2,1,0:T(8,128)(2,1)S(1)}, bf16[1,16,32,1152]{3,2,1,0:T(8,128)(2,1)}, u32[]{:S(2)}) copy-start(bf16[1,16,32,1152]{3,2,1,0:T(8,128)(2,1)} %param.22) | copy-start | bytes 3538948
  51.0 32.0 %copy-start.9 = (f32[1,4,1152]{2,1,0:T(4,128)S(1)}, f32[1,4,1152]{2,1,0:T(4,128)}, u32[]{:S(2)}) copy-start(f32[1,4,1152]{2,1,0:T(4,128)} %param.23) | copy-start | bytes 55300
  83.0 37.8 %copy-start.3 = (s32[4,32768]{1,0:T(4,128)S(1)}, s32[4,32768]{1,0:T(4,128)}, u32[]{:S(2)}) copy-start(s32[4,32768]{1,0:T(4,128)} %nodes_ref.1) | copy-start | bytes 1572868
  120.9 1.6 copy-start

commit v2 on v1

v2 whole, which is shorter than its diff:
```python
import functools

import jax
import jax.numpy as jnp
from jax import lax
from jax.experimental import pallas as pl
from jax.experimental.pallas import tpu as pltpu
from jax.sharding import PartitionSpec as P

ELEM_BLOCK = 2048
SHARE_ROWS = (0, 9)
SHARE_COUPLING = (9, 1)
SHARE_FLUX = (10, 2)
SHARE_BACK = (12, 4)
bf16 = jnp.bfloat16
f32 = jnp.float32
i32 = jnp.int32
MESH = pl.DeviceIdType.MESH
NT = (((1,), (1,)), ((), ()))
VMEM_LIMIT = 48 << 20


def iota(shape, dim):
    return lax.broadcasted_iota(i32, shape, dim)


def to_bf(x):
    return x.astype(f32).astype(bf16)


def onehot(rows, index):
    shape = (rows, index.shape[1])
    return jnp.where(
        to_bf(iota(shape, 0)) == jnp.broadcast_to(index, shape),
        jnp.ones((), bf16),
        jnp.zeros((), bf16),
    )


def split8(x):
    hi = x.astype(bf16).astype(f32)
    return jnp.where(iota(x.shape, 0) < 4, hi, x - hi)


def split_table(t):
    hi = t.astype(bf16)
    return jnp.concatenate([hi, (t - hi.astype(f32)).astype(bf16)], 1)


def pick(table, hot, q, groups):
    r = jnp.dot(table, jnp.concatenate([hot, hot], 0), preferred_element_type=f32)
    shape = (8, hot.shape[1])
    qh = jnp.broadcast_to(q, shape) - jnp.where(iota(shape, 0) >= 4, 1, 0)
    acc = jnp.where(qh == 0, r[0:8], 0.0)
    for j in range(1, groups):
        acc = jnp.where(qh == 2 * j, r[8 * j : 8 * j + 8], acc)
    return acc + pltpu.roll(acc, 4, axis=0)


def spread(part, q, groups):
    part = part.astype(bf16)
    p16 = jnp.concatenate([part, part], 0)
    qv = to_bf(jnp.broadcast_to(q, p16.shape) - jnp.where(iota(p16.shape, 0) >= 8, 1, 0))
    zero = jnp.zeros((), bf16)
    return jnp.concatenate(
        [jnp.where(qv == jnp.asarray(2 * j, bf16), p16, zero) for j in range(groups)], 0
    )


def elem_blocks(table, mats_ref, nodes_ref, out_ref, first, blocks):
    @pl.loop(first, first + blocks)
    def _(i):
        at = pl.ds(pl.multiple_of(i * ELEM_BLOCK, ELEM_BLOCK), ELEM_BLOCK)
        nodes = nodes_ref[:, at]
        hots, xs = [], []
        for a in range(4):
            n = nodes[a : a + 1]
            hot = onehot(256, to_bf(n & 255))
            hots.append(hot)
            xs.append(pick(table[...], hot, n >> 8, 18))
        total = None
        for b in range(4):
            c = mats_ref[0, pl.ds(b, 1), at] * xs[0]
            for a in range(1, 4):
                c = c + mats_ref[a, pl.ds(b, 1), at] * xs[a]
            d = lax.dot_general(
                spread(split8(c), (nodes[b : b + 1] >> 8) - 2, 16),
                hots[b],
                NT,
                preferred_element_type=f32,
            )
            total = d if total is None else total + d
        out_ref[...] += total


def bucket_kernel(count_ref, node_ref, block_ref, pos_ref, weight_ref, out_ref, acc, carry):
    step = pl.program_id(0)
    rb = node_ref.shape[1]

    @pl.when(step == 0)
    def _():
        acc[...] = jnp.zeros_like(acc)
        carry[...] = jnp.zeros_like(carry)

    node, pos, block = node_ref[...], pos_ref[...], block_ref[...]
    row = step * rb + iota((1, rb), 1)
    coef = jnp.where(row < count_ref[0], weight_ref[...], 0.0)
    bucket = (block & 7) * 16 + (block >> 3)

    owner = onehot(128, to_bf(bucket))
    upper = jnp.where(iota((256, 256), 0) <= iota((256, 256), 1), 1.0, 0.0).astype(bf16)
    before = carry[:, 0:1]
    ranks = []
    for at in range(0, rb, 256):
        hot = owner[:, at : at + 256]
        counts = jnp.dot(hot, upper, preferred_element_type=f32) + before
        ranks.append(jnp.sum(hot.astype(f32) * counts, axis=0, keepdims=True) - 1.0)
        before = counts[:, 255:256]
    carry[...] = jnp.broadcast_to(before, carry.shape)
    slot = onehot(256, jnp.concatenate(ranks, 1).astype(bf16))

    hi = coef.astype(bf16).astype(f32)
    sub = iota((8, rb), 0)
    part = jnp.zeros((8, rb), f32)
    highs = (pos >> 7).astype(f32), (node >> 8).astype(f32), hi
    lows = (pos & 127).astype(f32), (node & 255).astype(f32), coef - hi
    for i in range(3):
        part = jnp.where(sub == i, jnp.broadcast_to(highs[i], (8, rb)), part)
        part = jnp.where(sub == i + 4, jnp.broadcast_to(lows[i], (8, rb)), part)
    acc[...] += lax.dot_general(spread(part, bucket, 64), slot, NT, preferred_element_type=f32)

    @pl.when(step == pl.num_programs(0) - 1)
    def _():
        @pl.loop(0, 128)
        def _(b):
            c = acc[pl.ds(pl.multiple_of(b * 8, 8), 8), :]
            s = iota(c.shape, 0)
            c = c * jnp.where(s == 0, 128.0, jnp.where(s == 1, 256.0, 1.0))
            out_ref[b] = c + pltpu.roll(c, 4, axis=0)


def bucket_call(count, node, block, pos, weight):
    rows = node.shape[1]
    rb = 1024
    row_spec = pl.BlockSpec((1, rb), lambda i: (0, i))
    return pl.pallas_call(
        bucket_kernel,
        grid=(rows // rb,),
        in_specs=[pl.BlockSpec(memory_space=pltpu.SMEM)] + [row_spec] * 4,
        out_specs=pl.BlockSpec((128, 8, 256), lambda i: (0, 0, 0)),
        out_shape=jax.ShapeDtypeStruct((128, 8, 256), f32),
        scratch_shapes=[pltpu.VMEM((1024, 256), f32), pltpu.VMEM((128, 128), f32)],
        compiler_params=pltpu.CompilerParams(vmem_limit_bytes=VMEM_LIMIT),
        name="buckets",
    )(count, node, block, pos, weight)


DEVICES = 128


def place(index):
    wide = lax.axis_size("bem")
    return (index // wide, lax.rem(index, wide))


def greet_all(me):
    barrier = pltpu.get_barrier_semaphore()

    @pl.loop(1, DEVICES)
    def _(k):
        pl.semaphore_signal(
            barrier, inc=1, device_id=place(lax.rem(me + k, DEVICES)), device_id_type=MESH
        )


def await_all():
    pl.semaphore_wait(pltpu.get_barrier_semaphore(), DEVICES - 1)


def wait_bytes(ref, sem):
    pltpu.make_async_copy(ref, ref, sem).wait()


def send_chunks(me, send, got, sems, fill):
    group = 8

    def chunk(i, last):
        peers = [lax.rem(me + i * group + j + 1, DEVICES) for j in range(group)]
        fill(peers)
        for peer in peers[: group - 1] if last else peers:
            pltpu.make_async_remote_copy(
                src_ref=send.at[peer],
                dst_ref=got.at[me],
                send_sem=sems.at[0],
                recv_sem=sems.at[1],
                device_id=place(peer),
                device_id_type=MESH,
            ).start()

    @pl.loop(0, DEVICES // group - 1)
    def _(i):
        chunk(i, False)

    chunk(DEVICES // group - 1, True)
    got[me] = send[me]


def wait_chunks(send, got, sems):
    most = pl.ds(0, DEVICES - 1)
    wait_bytes(send.at[most], sems.at[0])
    wait_bytes(got.at[most], sems.at[1])


def device_index():
    return lax.axis_index("fem") * lax.axis_size("bem") + lax.axis_index("bem")


def rows_kernel(
    slots_ref, field_ref, mats_ref, nodes_ref, got, stiff_ref, table, own, halo, send, sems, halo_sems
):
    me = device_index()
    greet_all(me)
    own[...] = split_table(field_ref[...])
    stiff_ref[...] = jnp.zeros_like(stiff_ref)
    await_all()

    right, left = lax.rem(me + 1, DEVICES), lax.rem(me + DEVICES - 1, DEVICES)
    up = pltpu.make_async_remote_copy(
        src_ref=field_ref.at[pl.ds(120, 8)],
        dst_ref=halo.at[0],
        send_sem=halo_sems.at[0],
        recv_sem=halo_sems.at[1],
        device_id=place(right),
        device_id_type=MESH,
    )
    down = pltpu.make_async_remote_copy(
        src_ref=field_ref.at[pl.ds(0, 8)],
        dst_ref=halo.at[1],
        send_sem=halo_sems.at[2],
        recv_sem=halo_sems.at[3],
        device_id=place(left),
        device_id_type=MESH,
    )
    up.start()
    down.start()

    def fill(peers):
        tiles = [slots_ref[p] for p in peers]
        node = jnp.concatenate([t[1:2] for t in tiles], 1).astype(i32)
        coef = jnp.concatenate([t[2:3] for t in tiles], 1)
        x = pick(own[...], onehot(256, to_bf(node & 255)), node >> 8, 16) * coef
        for j, p in enumerate(peers):
            send[p, 0:4] = x[0:4, 256 * j : 256 * j + 256]
            send[p, 4:5] = tiles[j][0:1]

    send_chunks(me, send, got, sems, fill)

    up.wait()
    down.wait()
    low = jnp.where(me == 0, 0.0, halo[0])
    high = jnp.where(me == DEVICES - 1, 0.0, halo[1])
    table[0:8] = split_table(low)
    table[8:136] = own[...]
    table[136:144] = split_table(high)
    elem_blocks(table, mats_ref, nodes_ref, stiff_ref, *SHARE_ROWS)
    wait_chunks(send, got, sems)


def rows_call(slots, field, mats, nodes):
    vmem = pl.BlockSpec(memory_space=pltpu.VMEM)
    return pl.pallas_call(
        rows_kernel,
        in_specs=[vmem] * 4,
        out_specs=[vmem] * 3,
        out_shape=[
            jax.ShapeDtypeStruct((DEVICES, 5, 256), f32),
            jax.ShapeDtypeStruct((256, 256), f32),
            jax.ShapeDtypeStruct((144, 512), bf16),
        ],
        scratch_shapes=[
            pltpu.VMEM((128, 512), bf16),
            pltpu.VMEM((2, 8, 256), f32),
            pltpu.VMEM((DEVICES, 5, 256), f32),
            pltpu.SemaphoreType.DMA((2,)),
            pltpu.SemaphoreType.DMA((4,)),
        ],
        compiler_params=pltpu.CompilerParams(
            collective_id=0, has_side_effects=True, vmem_limit_bytes=VMEM_LIMIT
        ),
        name="rows_out",
    )(slots, field, mats, nodes)


def flux_kernel(
    got_ref,
    left_ref,
    near_ref,
    right_ref,
    field_ref,
    table,
    mats_ref,
    nodes_ref,
    out_ref,
    stiff_ref,
    acc,
    part_ref,
    near_out,
    parts,
    shares,
    sums,
    sems,
):
    fems, bems = 8, 16
    f, b = lax.axis_index("fem"), lax.axis_index("bem")
    barrier = pltpu.get_barrier_semaphore()
    for k in range(1, fems):
        pl.semaphore_signal(
            barrier, inc=1, device_id=(lax.rem(f + k, fems), b), device_id_type=MESH
        )
    for k in range(1, bems):
        pl.semaphore_signal(
            barrier, inc=1, device_id=(f, lax.rem(b + k, bems)), device_id_type=MESH
        )
    acc[...] = jnp.zeros_like(acc)
    stiff_ref[...] = jnp.zeros_like(stiff_ref)
    group = 16

    @pl.loop(0, DEVICES // group)
    def _(i):
        tiles = [got_ref[i * group + j] for j in range(group)]
        vals = jnp.concatenate([t[0:4] for t in tiles], 1)
        pos = jnp.concatenate([t[4:5] for t in tiles], 1).astype(i32)
        acc[...] += lax.dot_general(
            spread(split8(jnp.concatenate([vals, vals], 0)), pos >> 7, 5),
            onehot(128, to_bf(pos & 127)),
            NT,
            preferred_element_type=f32,
        )

    pieces = []
    for t in range(9):
        a = acc[8 * t : 8 * t + 8]
        piece = split8(a + pltpu.roll(a, 4, axis=0)).astype(bf16)
        pieces.append(piece)
        n = jnp.dot(piece, near_ref[t], preferred_element_type=f32)
        near_out[:, 128 * t : 128 * t + 128] = (n + pltpu.roll(n, 4, axis=0))[0:4]
    c = lax.dot_general(jnp.concatenate(pieces, 1), left_ref[...], NT, preferred_element_type=f32)
    part_ref[...] = (c + pltpu.roll(c, 4, axis=0))[0:4]

    pl.semaphore_wait(barrier, fems + bems - 2)
    for k in range(1, fems):
        pltpu.make_async_remote_copy(
            src_ref=part_ref,
            dst_ref=parts.at[f],
            send_sem=sems.at[0],
            recv_sem=sems.at[1],
            device_id=(lax.rem(f + k, fems), b),
            device_id_type=MESH,
        ).start()
    parts[f] = part_ref[...]
    elem_blocks(table, mats_ref, nodes_ref, stiff_ref, *SHARE_COUPLING)
    most = parts.at[pl.ds(0, fems - 1)]
    wait_bytes(most, sems.at[0])
    wait_bytes(most, sems.at[1])

    total = parts[0]
    for k in range(1, fems):
        total = total + parts[k]
    for half in range(2):
        c = total[:, 256 * half : 256 * half + 256]
        c = split8(jnp.concatenate([c, c], 0))
        stacked = jnp.concatenate([c] * 8, 0)
        shape = stacked.shape
        diag = jnp.where((iota(shape, 0) >> 3) == (iota(shape, 1) >> 5), stacked, 0.0).astype(bf16)
        far = jnp.dot(
            diag, right_ref[256 * half : 256 * half + 256], preferred_element_type=f32
        )
        for s in range(8):
            a = far[8 * s : 8 * s + 8]
            shares[8 * half + s] = (a + pltpu.roll(a, 4, axis=0))[0:4]
    shares[b] = shares[b] + near_out[...]

    for k in range(1, bems):
        peer = lax.rem(b + k, bems)
        pltpu.make_async_remote_copy(
            src_ref=shares.at[peer],
            dst_ref=sums.at[b],
            send_sem=sems.at[2],
            recv_sem=sems.at[3],
            device_id=(f, peer),
            device_id_type=MESH,
        ).start()
    sums[b] = shares[b]
    elem_blocks(table, mats_ref, nodes_ref, stiff_ref, *SHARE_FLUX)
    most = sums.at[pl.ds(0, bems - 1)]
    wait_bytes(most, sems.at[2])
    wait_bytes(most, sems.at[3])
    flux = field_ref[...]
    for k in range(bems):
        flux = flux + sums[k]
    out_ref[...] = flux


def flux_call(*args):
    vmem = pl.BlockSpec(memory_space=pltpu.VMEM)
    return pl.pallas_call(
        flux_kernel,
        in_specs=[vmem] * 8,
        out_specs=[vmem] * 2,
        out_shape=[jax.ShapeDtypeStruct((4, 1152), f32), jax.ShapeDtypeStruct((256, 256), f32)],
        scratch_shapes=[
            pltpu.VMEM((80, 128), f32),
            pltpu.VMEM((4, 512), f32),
            pltpu.VMEM((4, 1152), f32),
            pltpu.VMEM((8, 4, 512), f32),
            pltpu.VMEM((16, 4, 1152), f32),
            pltpu.VMEM((16, 4, 1152), f32),
            pltpu.SemaphoreType.DMA((4,)),
        ],
        compiler_params=pltpu.CompilerParams(
            collective_id=1, has_side_effects=True, vmem_limit_bytes=VMEM_LIMIT
        ),
        name="flux",
    )(*args)


def back_kernel(
    flux_ref, rows_ref, table, mats_ref, nodes_ref, got, stiff_ref, flux_f32, flux_table, send, sems
):
    me = device_index()
    greet_all(me)
    flux_f32[...] = jnp.zeros_like(flux_f32)
    for t in range(9):
        flux_f32[4 * t : 4 * t + 4] = flux_ref[:, 128 * t : 128 * t + 128]
    flux_table[...] = split_table(flux_f32[...])
    stiff_ref[...] = jnp.zeros_like(stiff_ref)
    await_all()

    def fill(peers):
        pos = jnp.concatenate([rows_ref[p, 4:5] for p in peers], 1).astype(i32)
        x = pick(flux_table[...], onehot(128, to_bf(pos & 127)), pos >> 7, 5)
        for j, p in enumerate(peers):
            send[p] = x[0:4, 256 * j : 256 * j + 256]

    send_chunks(me, send, got, sems, fill)
    elem_blocks(table, mats_ref, nodes_ref, stiff_ref, *SHARE_BACK)
    wait_chunks(send, got, sems)


def back_call(*args):
    vmem = pl.BlockSpec(memory_space=pltpu.VMEM)
    return pl.pallas_call(
        back_kernel,
        in_specs=[vmem] * 5,
        out_specs=[vmem] * 2,
        out_shape=[
            jax.ShapeDtypeStruct((DEVICES, 4, 256), f32),
            jax.ShapeDtypeStruct((256, 256), f32),
        ],
        scratch_shapes=[
            pltpu.VMEM((40, 128), f32),
            pltpu.VMEM((40, 256), bf16),
            pltpu.VMEM((DEVICES, 4, 256), f32),
            pltpu.SemaphoreType.DMA((2,)),
        ],
        compiler_params=pltpu.CompilerParams(
            collective_id=2, has_side_effects=True, vmem_limit_bytes=VMEM_LIMIT
        ),
        name="flux_back",
    )(*args)


def nodes_kernel(stiff_a, stiff_b, stiff_c, flux_ref, slots_ref, out_ref, acc):
    step = pl.program_id(0)

    @pl.when(step == 0)
    def _():
        acc[...] = stiff_a[...] + stiff_b[...] + stiff_c[...]

    count = flux_ref.shape[0]
    node = jnp.concatenate([slots_ref[s, 1:2] for s in range(count)], 1).astype(i32)
    coef = jnp.concatenate([slots_ref[s, 2:3] for s in range(count)], 1)
    x = jnp.concatenate([flux_ref[s] for s in range(count)], 1)
    x = jnp.concatenate([x, x], 0) * coef
    acc[...] += lax.dot_general(
        spread(split8(x), node >> 8, 16),
        onehot(256, to_bf(node & 255)),
        NT,
        preferred_element_type=f32,
    )

    @pl.when(step == pl.num_programs(0) - 1)
    def _():
        for q in range(32):
            a = acc[8 * q : 8 * q + 8]
            out_ref[:, 256 * q : 256 * q + 256] = (a + pltpu.roll(a, 4, axis=0))[0:4]


def nodes_call(stiffs, flux, slots):
    sb = 16
    whole = pl.BlockSpec((256, 256), lambda i: (0, 0))
    return pl.pallas_call(
        nodes_kernel,
        grid=(DEVICES // sb,),
        in_specs=[whole] * 3
        + [
            pl.BlockSpec((sb, 4, 256), lambda i: (i, 0, 0)),
            pl.BlockSpec((sb, 8, 256), lambda i: (i, 0, 0)),
        ],
        out_specs=pl.BlockSpec((4, 8192), lambda i: (0, 0)),
        out_shape=jax.ShapeDtypeStruct((4, 8192), f32),
        scratch_shapes=[pltpu.VMEM((256, 256), f32)],
        compiler_params=pltpu.CompilerParams(vmem_limit_bytes=VMEM_LIMIT),
        name="nodes",
    )(*stiffs, flux, slots)


def tiles(x, width):
    return x.reshape(4, -1, width).transpose(1, 0, 2).reshape(-1, width)


def per_device(
    fem_field,
    elem_mats,
    elem_nodes,
    trace_count,
    trace_node,
    trace_block,
    trace_pos,
    trace_weight,
    near_tiles,
    left_basis,
    right_basis,
    bem_field,
):
    slots = bucket_call(
        trace_count,
        trace_node.reshape(1, -1),
        trace_block.reshape(1, -1),
        trace_pos.reshape(1, -1),
        trace_weight.reshape(1, -1),
    )
    got, stiff_a, table = rows_call(slots, tiles(fem_field, 256), elem_mats, elem_nodes)
    flux, stiff_b = flux_call(
        got,
        left_basis.reshape(512, 1152),
        near_tiles[0],
        right_basis.reshape(512, 1152),
        bem_field[0],
        table,
        elem_mats,
        elem_nodes,
    )
    returned, stiff_c = back_call(flux, got, table, elem_mats, elem_nodes)
    out = nodes_call((stiff_a, stiff_b, stiff_c), returned, slots)
    return out, flux[None]


def solution(mesh):
    placed = (
        P(None, ("fem", "bem")),
        P(None, None, ("fem", "bem")),
        P(None, ("fem", "bem")),
        P(("fem", "bem")),
        P(("fem", "bem")),
        P(("fem", "bem"), None),
        P(("fem", "bem")),
        P(("fem", "bem")),
        P("bem", "fem", None, None),
        P("bem", None, None, "fem"),
        P("bem", None, None, "fem"),
        P("bem", None, "fem"),
    )
    return jax.shard_map(
        per_device,
        mesh=mesh,
        in_specs=placed,
        out_specs=(P(None, ("fem", "bem")), P("bem", None, "fem")),
        check_vma=False,
    )
```

time: 197 us -> 116 us (0.59)
  Pallas kernels: 176 us -> 109 us
  starting transfers between devices: 11.2 us -> 0 us
    pallas_call x7 -> x4, Pallas kernels: 142 us -> 90 us  [the longest x1 43.5 us: rows_call(): pl.pallas_call(rows_kernel, in_specs=[vmem] * 4, out_specs=[vmem] * 3, ou...]
    pallas_call x1, Pallas kernels: 33.6 us -> 18.5 us  [bucket_call(): pl.pallas_call(bucket_kernel, grid=(rows // rb,), in_specs=[pl.BlockSpec(...]
    ppermute x2 -> x0, starting transfers between devices: 11.2 us -> none  [the longest x1 9.24 us: per_device(): high = lax.ppermute(fem_field[:, :REACH], both, back)]
    unnamed x21 -> x25, local copies, waits for them, and re-layouts: 2.25 us -> 5.57 us
    reshape x2 -> x0, local copies, waits for them, and re-layouts: 3.11 us -> none  [the longest x1 3.03 us: per_device(): stiff = elem_call(table, elem_mats.reshape(16, -1), elem_nodes)]
  transfers between devices with their start and end apart: 2 -> 0, of which waited for: 0 -> 0; matrix products, arithmetic and copies ran while one was open for 2% -> 0% of each run, Pallas kernels for 52% -> 0%
where the time goes in v2:
time: 116 us
  Pallas kernels  109 us (94%)
  local copies, waits for them, and re-layouts  5.62 us (5%)
  between operations  1.47 us (1%)
    pallas_call x1, Pallas kernels, rows_call(): pl.pallas_call(rows_kernel, in_specs=[vmem] * 4, out_specs=[vmem] * 3, ou...  43.5 us
    pallas_call x1, Pallas kernels, back_call(): pl.pallas_call(back_kernel, in_specs=[vmem] * 5, out_specs=[vmem] * 2, ou...  23.6 us
    pallas_call x1, Pallas kernels, bucket_call(): pl.pallas_call(bucket_kernel, grid=(rows // rb,), in_specs=[pl.BlockSpec(...  18.5 us
    pallas_call x1, Pallas kernels, flux_call(): pl.pallas_call(flux_kernel, in_specs=[vmem] * 8, out_specs=[vmem] * 2, ou...  16.1 us
    pallas_call x1, Pallas kernels, nodes_call(): pl.pallas_call(nodes_kernel, grid=(DEVICES // sb,), in_specs=[whole] * 3...  6.85 us
    unnamed x25, local copies, waits for them, and re-layouts  5.57 us

profile of v2, /device:TPU:1, one launch (start us, length us, event | category | flops | bytes accessed | tf_op | source)
XLA Modules:
  0.0 115.6 jit_solution(9940806893932844891)
XLA Ops:
  0.6 0.0 copy-start.2
  1.3 0.0 copy-start.6
  1.4 0.8 copy-done.6
  2.2 0.0 copy-start.7
  2.2 0.8 copy-done.7
  3.0 0.0 copy-start.8
  3.0 0.8 copy-done.8
  3.9 0.0 copy-start.9
  3.9 0.8 copy-done.9
  4.7 0.0 copy-start.11
  4.7 18.5 %buckets.1.slots_ref = f32[128,8,256]{2,1,0:T(8,128)S(1)} custom-call(s32[1]{0:T(128)S(6)} %copy.16.count_ref, s32[1,16384]{1,0:T(1,128)S(1)} %bitcast.16, s32[1,16384]{1,0:T(1,128)S(1)} %bitcast.17, s32[1,16384]{1,0:T(1,128)S(1)} %bitcast.18, f32[1,16384]{1,0:T(1,128)S(1)} %bitcast.19), custom_call_target="tpu_custom_call" | custom-call | tf_op jit(solution)/shard_map/buckets/pallas_call | solution.py:146
  23.2 0.0 copy-done.11
  23.3 0.0 copy-done.2
  23.3 0.0 copy-start
  23.3 1.6 %copy-done = f32[4,4,32768]{2,1,0:T(4,128)S(1)} copy-done((f32[4,4,32768]{2,1,0:T(4,128)S(1)}, f32[4,4,32768]{2,1,0:T(4,128)}, u32[]{:S(2)}) %copy-start) | copy-done | bytes 2097176
  24.9 0.0 copy-start.3
  24.9 0.0 copy-start.4
  24.9 0.0 copy-start.5
  24.9 0.0 copy-start.10
  24.9 43.5 %rows_out.1 = (f32[128,5,256]{2,1,0:T(8,128)S(1)}, f32[256,256]{1,0:T(8,128)S(1)}, bf16[144,512]{1,0:T(8,128)(2,1)S(1)}) custom-call(f32[128,8,256]{2,1,0:T(8,128)S(1)} %buckets.1.slots_ref, f32[128,256]{1,0:T(8,128)S(1)} %reshape.33.field_ref, f32[4,4,32768]{2,1,0:T(4,128)S(1)} %copy-done, s32[4,32768]{1,0:T(4,128)S(1)} %copy-done.2), custom_call_target="tpu_custom_call" | custom-call | tf_op jit(solution)/shard_map/rows_out/pallas_call | solution.py:271
  68.4 0.0 copy-done.3
  68.5 0.0 copy-done.4
  68.5 0.0 copy-done.5
  68.5 0.0 copy-done.10
  68.5 0.0 copy-start.1
  68.5 16.1 %flux.1 = (f32[4,1152]{1,0:T(4,128)S(1)}, f32[256,256]{1,0:T(8,128)S(1)}) custom-call(f32[128,5,256]{2,1,0:T(8,128)S(1)} %get-tuple-element.10.got_ref.rows_ref, bf16[512,1152]{1,0:T(8,128)(2,1)S(1)} %bitcast.12, bf16[9,128,128]{2,1,0:T(8,128)(2,1)S(1)} %bitcast.14, bf16[512,1152]{1,0:T(8,128)(2,1)S(1)} %bitcast.13, f32[4,1152]{1,0:T(4,128)S(1)} %bitcast.20, ...), custom_call_target="tpu_custom_call" | custom-call | tf_op jit(solution)/shard_map/flux/pallas_call | solution.py:406
  84.6 0.0 copy-done.1
  84.6 23.6 %flux_back.1 = (f32[128,4,256]{2,1,0:T(4,128)S(1)}, f32[256,256]{1,0:T(8,128)S(1)}) custom-call(f32[4,1152]{1,0:T(4,128)S(1)} %get-tuple-element.13.flux_ref, f32[128,5,256]{2,1,0:T(8,128)S(1)} %get-tuple-element.10.got_ref.rows_ref, bf16[144,512]{1,0:T(8,128)(2,1)S(1)} %get-tuple-element.11.table, f32[4,4,32768]{2,1,0:T(4,128)S(1)} %copy-done.1, ...), custom_call_target="tpu_custom_call" | custom-call | tf_op jit(solution)/shard_map/flux_back/pallas_call | solution.py:452
  108.2 6.8 %nodes.1 = f32[4,8192]{1,0:T(4,128)} custom-call(f32[256,256]{1,0:T(8,128)S(1)} %get-tuple-element.9.stiff_a, f32[256,256]{1,0:T(8,128)S(1)} %get-tuple-element.12.stiff_b, f32[256,256]{1,0:T(8,128)S(1)} %get-tuple-element.14.stiff_c, f32[128,4,256]{2,1,0:T(4,128)S(1)} %get-tuple-element.15.flux_ref, f32[128,8,256]{2,1,0:T(8,128)S(1)} %buckets.1.slots_ref), custom_call_target="tpu_custom_call" | custom-call | tf_op jit(solution)/shard_map/nodes/pallas_call | solution.py:502
  115.0 0.6 copy.17
  (1 shorter events, 0.0 us)
Async XLA Ops:
  0.6 22.7 %copy-start.2 = (s32[4,32768]{1,0:T(4,128)S(1)}, s32[4,32768]{1,0:T(4,128)}, u32[]{:S(2)}) copy-start(s32[4,32768]{1,0:T(4,128)} %nodes_ref.5) | copy-start | bytes 1572868
  1.3 0.8 copy-start.6
  2.2 0.8 copy-start.7
  3.0 0.8 copy-start.8
  3.9 0.8 copy-start.9
  4.7 18.5 %copy-start.11 = (f32[4,8192]{1,0:T(4,128)S(1)}, f32[4,8192]{1,0:T(4,128)}, u32[]{:S(2)}) copy-start(f32[4,8192]{1,0:T(4,128)} %param.12) | copy-start | bytes 393220
  23.3 1.6 %copy-start = (f32[4,4,32768]{2,1,0:T(4,128)S(1)}, f32[4,4,32768]{2,1,0:T(4,128)}, u32[]{:S(2)}) copy-start(f32[4,4,32768]{2,1,0:T(4,128)} %mats_ref.5) | copy-start | bytes 6291460
  24.9 43.5 %copy-start.3 = (bf16[1,16,32,1152]{3,2,1,0:T(8,128)(2,1)S(1)}, bf16[1,16,32,1152]{3,2,1,0:T(8,128)(2,1)}, u32[]{:S(2)}) copy-start(bf16[1,16,32,1152]{3,2,1,0:T(8,128)(2,1)} %param.21) | copy-start | bytes 3538948
  24.9 43.5 %copy-start.4 = (bf16[1,16,32,1152]{3,2,1,0:T(8,128)(2,1)S(1)}, bf16[1,16,32,1152]{3,2,1,0:T(8,128)(2,1)}, u32[]{:S(2)}) copy-start(bf16[1,16,32,1152]{3,2,1,0:T(8,128)(2,1)} %param.22) | copy-start | bytes 3538948
  24.9 43.5 %copy-start.5 = (bf16[1,9,128,128]{3,2,1,0:T(8,128)(2,1)S(1)}, bf16[1,9,128,128]{3,2,1,0:T(8,128)(2,1)}, u32[]{:S(2)}) copy-start(bf16[1,9,128,128]{3,2,1,0:T(8,128)(2,1)} %param.20) | copy-start | bytes 884740
  24.9 43.6 %copy-start.10 = (f32[1,4,1152]{2,1,0:T(4,128)S(1)}, f32[1,4,1152]{2,1,0:T(4,128)}, u32[]{:S(2)}) copy-start(f32[1,4,1152]{2,1,0:T(4,128)} %param.23) | copy-start | bytes 55300
  68.5 16.1 %copy-start.1 = (f32[4,4,32768]{2,1,0:T(4,128)S(1)}, f32[4,4,32768]{2,1,0:T(4,128)}, u32[]{:S(2)}) copy-start(f32[4,4,32768]{2,1,0:T(4,128)} %mats_ref.5) | copy-start | bytes 6291460

commit v3 on v0

v3 whole, which is shorter than its diff:
```python
import functools

import jax
import jax.numpy as jnp
from jax import lax
from jax.experimental import pallas as pl
from jax.experimental.pallas import tpu as pltpu
from jax.sharding import PartitionSpec as P

ELEM_BLOCK = 2048
ROW_BLOCK = 2048
SHARE_ROWS = (0, 6)
SHARE_COUPLING = (6, 2)
SHARE_FLUX = (8, 3)
SHARE_BACK = (11, 5)
bf16 = jnp.bfloat16
f32 = jnp.float32
i32 = jnp.int32
MESH = pl.DeviceIdType.MESH
NT = (((1,), (1,)), ((), ()))
VMEM_LIMIT = 63 << 20


def iota(shape, dim):
    return lax.broadcasted_iota(i32, shape, dim)


def to_bf(x):
    return x.astype(f32).astype(bf16)


def onehot(rows, index):
    shape = (rows, index.shape[1])
    return jnp.where(
        to_bf(iota(shape, 0)) == jnp.broadcast_to(index, shape),
        jnp.ones((), bf16),
        jnp.zeros((), bf16),
    )


def split8(x):
    hi = x.astype(bf16).astype(f32)
    return jnp.where(iota(x.shape, 0) < 4, hi, x - hi)


def split_table(t):
    hi = t.astype(bf16)
    return jnp.concatenate([hi, (t - hi.astype(f32)).astype(bf16)], 1)


def pick(table, hot, q, groups):
    r = jnp.dot(table, jnp.concatenate([hot, hot], 0), preferred_element_type=f32)
    shape = (8, hot.shape[1])
    qh = jnp.broadcast_to(q, shape) - jnp.where(iota(shape, 0) >= 4, 1, 0)
    acc = jnp.where(qh == 0, r[0:8], 0.0)
    for j in range(1, groups):
        acc = jnp.where(qh == 2 * j, r[8 * j : 8 * j + 8], acc)
    return acc + pltpu.roll(acc, 4, axis=0)


def spread(part, q, groups):
    part = part.astype(bf16)
    p16 = jnp.concatenate([part, part], 0)
    qv = to_bf(jnp.broadcast_to(q, p16.shape) - jnp.where(iota(p16.shape, 0) >= 8, 1, 0))
    zero = jnp.zeros((), bf16)
    return jnp.concatenate(
        [jnp.where(qv == jnp.asarray(2 * j, bf16), p16, zero) for j in range(groups)], 0
    )


def elem_blocks(table, mats_ref, nodes_ref, out_ref, first, blocks):
    @pl.loop(first, first + blocks)
    def _(i):
        at = pl.ds(pl.multiple_of(i * ELEM_BLOCK, ELEM_BLOCK), ELEM_BLOCK)
        nodes = nodes_ref[:, at]
        hots, xs = [], []
        for a in range(4):
            n = nodes[a : a + 1]
            hot = onehot(256, to_bf(n & 255))
            hots.append(hot)
            xs.append(pick(table[...], hot, n >> 8, 18))
        total = None
        for b in range(4):
            c = mats_ref[0, pl.ds(b, 1), at] * xs[0]
            for a in range(1, 4):
                c = c + mats_ref[a, pl.ds(b, 1), at] * xs[a]
            d = lax.dot_general(
                spread(split8(c), (nodes[b : b + 1] >> 8) - 2, 16),
                hots[b],
                NT,
                preferred_element_type=f32,
            )
            total = d if total is None else total + d
        out_ref[...] += total


def bucket_rows(count_ref, node_ref, block_ref, pos_ref, weight_ref, out_ref, acc):
    rb = ROW_BLOCK
    acc[...] = jnp.zeros_like(acc)

    def step(i, before):
        at = pl.ds(pl.multiple_of(i * rb, rb), rb)
        node, pos, block = node_ref[:, at], pos_ref[:, at], block_ref[:, at]
        row = i * rb + iota((1, rb), 1)
        coef = jnp.where(row < count_ref[0], weight_ref[:, at], 0.0)
        bucket = (block & 7) * 16 + (block >> 3)

        owner = onehot(128, to_bf(bucket))
        upper = jnp.where(iota((256, 256), 0) <= iota((256, 256), 1), 1.0, 0.0).astype(bf16)
        ranks = []
        for k in range(0, rb, 256):
            hot = owner[:, k : k + 256]
            counts = jnp.dot(hot, upper, preferred_element_type=f32) + before
            ranks.append(jnp.sum(hot.astype(f32) * counts, axis=0, keepdims=True) - 1.0)
            before = counts[:, 255:256]
        slot = onehot(256, jnp.concatenate(ranks, 1).astype(bf16))

        hi = coef.astype(bf16).astype(f32)
        sub = iota((8, rb), 0)
        part = jnp.zeros((8, rb), f32)
        highs = (pos >> 7).astype(f32), (node >> 8).astype(f32), hi
        lows = (pos & 127).astype(f32), (node & 255).astype(f32), coef - hi
        for k in range(3):
            part = jnp.where(sub == k, jnp.broadcast_to(highs[k], (8, rb)), part)
            part = jnp.where(sub == k + 4, jnp.broadcast_to(lows[k], (8, rb)), part)
        acc[...] += lax.dot_general(
            spread(part, bucket, 64), slot, NT, preferred_element_type=f32
        )
        return before

    lax.fori_loop(0, node_ref.shape[1] // rb, step, jnp.zeros((128, 1), f32))

    @pl.loop(0, 128)
    def _(b):
        c = acc[pl.ds(pl.multiple_of(b * 8, 8), 8), :]
        s = iota(c.shape, 0)
        c = c * jnp.where(s == 0, 128.0, jnp.where(s == 1, 256.0, 1.0))
        out_ref[b] = c + pltpu.roll(c, 4, axis=0)


DEVICES = 128


def place(index):
    wide = lax.axis_size("bem")
    return (index // wide, lax.rem(index, wide))


def greet_all(me):
    barrier = pltpu.get_barrier_semaphore()

    @pl.loop(1, DEVICES)
    def _(k):
        pl.semaphore_signal(
            barrier, inc=1, device_id=place(lax.rem(me + k, DEVICES)), device_id_type=MESH
        )


def await_all():
    pl.semaphore_wait(pltpu.get_barrier_semaphore(), DEVICES - 1)


def remote(src, dst, sems, at, device):
    return pltpu.make_async_remote_copy(
        src_ref=src,
        dst_ref=dst,
        send_sem=sems.at[at],
        recv_sem=sems.at[at + 1],
        device_id=device,
        device_id_type=MESH,
    )


def wait_bytes(ref, sem):
    pltpu.make_async_copy(ref, ref, sem).wait()


def send_chunks(me, send, got, sems, at, fill):
    group = 8

    def chunk(i, last):
        peers = [lax.rem(me + i * group + j + 1, DEVICES) for j in range(group)]
        fill(peers)
        for peer in peers[: group - 1] if last else peers:
            remote(send.at[peer], got.at[me], sems, at, place(peer)).start()

    @pl.loop(0, DEVICES // group - 1)
    def _(i):
        chunk(i, False)

    chunk(DEVICES // group - 1, True)
    got[me] = send[me]


def wait_copies(ref, count, sems, at):
    most = ref.at[pl.ds(0, count - 1)]
    wait_bytes(most, sems.at[at])
    wait_bytes(most, sems.at[at + 1])


def sum_rows(got, left, near, acc, near_out, part_ref):
    acc[...] = jnp.zeros_like(acc)
    group = 16

    @pl.loop(0, DEVICES // group)
    def _(i):
        tiles = [got[i * group + j] for j in range(group)]
        vals = jnp.concatenate([t[0:4] for t in tiles], 1)
        pos = jnp.concatenate([t[4:5] for t in tiles], 1).astype(i32)
        acc[...] += lax.dot_general(
            spread(split8(jnp.concatenate([vals, vals], 0)), pos >> 7, 5),
            onehot(128, to_bf(pos & 127)),
            NT,
            preferred_element_type=f32,
        )

    pieces = []
    for t in range(9):
        a = acc[8 * t : 8 * t + 8]
        piece = split8(a + pltpu.roll(a, 4, axis=0)).astype(bf16)
        pieces.append(piece)
        n = jnp.dot(piece, near[t], preferred_element_type=f32)
        near_out[:, 128 * t : 128 * t + 128] = (n + pltpu.roll(n, 4, axis=0))[0:4]
    c = lax.dot_general(jnp.concatenate(pieces, 1), left[...], NT, preferred_element_type=f32)
    part_ref[...] = (c + pltpu.roll(c, 4, axis=0))[0:4]


def far_field(parts, right, shares):
    total = parts[0]
    for k in range(1, parts.shape[0]):
        total = total + parts[k]
    for half in range(2):
        c = total[:, 256 * half : 256 * half + 256]
        c = split8(jnp.concatenate([c, c], 0))
        stacked = jnp.concatenate([c] * 8, 0)
        shape = stacked.shape
        diag = jnp.where((iota(shape, 0) >> 3) == (iota(shape, 1) >> 5), stacked, 0.0).astype(bf16)
        far = jnp.dot(diag, right[256 * half : 256 * half + 256], preferred_element_type=f32)
        for s in range(8):
            a = far[8 * s : 8 * s + 8]
            shares[8 * half + s] = (a + pltpu.roll(a, 4, axis=0))[0:4]


def add_returned(got, slots, acc):
    group = 16

    @pl.loop(0, DEVICES // group)
    def _(i):
        at = [i * group + j for j in range(group)]
        node = jnp.concatenate([slots[s, 1:2] for s in at], 1).astype(i32)
        coef = jnp.concatenate([slots[s, 2:3] for s in at], 1)
        x = jnp.concatenate([got[s] for s in at], 1)
        x = jnp.concatenate([x, x], 0) * coef
        acc[...] += lax.dot_general(
            spread(split8(x), node >> 8, 16),
            onehot(256, to_bf(node & 255)),
            NT,
            preferred_element_type=f32,
        )


def whole_kernel(
    count_ref,
    field_hbm,
    node_hbm,
    block_hbm,
    pos_hbm,
    weight_hbm,
    bem_hbm,
    mats_hbm,
    nodes_hbm,
    left_hbm,
    near_hbm,
    right_hbm,
    fem_out,
    flux_out,
    field,
    node_ref,
    block_ref,
    pos_ref,
    weight_ref,
    bem_ref,
    field_ref,
    mats,
    nodes,
    left,
    near,
    right,
    bucket_acc,
    slots,
    table,
    own,
    halo,
    send,
    got,
    row_acc,
    part_ref,
    near_out,
    parts,
    shares,
    sums,
    flux_f32,
    flux_table,
    send_back,
    got_back,
    stiff,
    sems,
    local_sems,
):
    fems, bems = lax.axis_size("fem"), lax.axis_size("bem")
    f, b = lax.axis_index("fem"), lax.axis_index("bem")
    me = f * bems + b
    pairs = [
        (block_hbm, block_ref),
        (node_hbm, node_ref),
        (pos_hbm, pos_ref),
        (weight_hbm, weight_ref),
        (field_hbm, field),
        (nodes_hbm, nodes),
        (mats_hbm, mats),
        (left_hbm, left),
        (near_hbm, near),
        (right_hbm, right),
        (bem_hbm, bem_ref),
    ]
    loads = [
        pltpu.make_async_copy(src, dst, local_sems.at[k]) for k, (src, dst) in enumerate(pairs)
    ]
    for load in loads:
        load.start()
    greet_all(me)
    stiff[...] = jnp.zeros_like(stiff)
    for load in loads[:5]:
        load.wait()
    for q in range(32):
        field_ref[4 * q : 4 * q + 4] = field[:, 256 * q : 256 * q + 256]
    own[...] = split_table(field_ref[...])
    bucket_rows(count_ref, node_ref, block_ref, pos_ref, weight_ref, slots, bucket_acc)

    await_all()
    up = remote(
        field_ref.at[pl.ds(120, 8)], halo.at[0], sems, 0, place(lax.rem(me + 1, DEVICES))
    )
    down = remote(
        field_ref.at[pl.ds(0, 8)], halo.at[1], sems, 2, place(lax.rem(me + DEVICES - 1, DEVICES))
    )
    up.start()
    down.start()

    def fill_rows(peers):
        parts8 = [slots[p] for p in peers]
        node = jnp.concatenate([t[1:2] for t in parts8], 1).astype(i32)
        coef = jnp.concatenate([t[2:3] for t in parts8], 1)
        x = pick(own[...], onehot(256, to_bf(node & 255)), node >> 8, 16) * coef
        for j, p in enumerate(peers):
            send[p, 0:4] = x[0:4, 256 * j : 256 * j + 256]
            send[p, 4:5] = parts8[j][0:1]

    send_chunks(me, send, got, sems, 4, fill_rows)

    up.wait()
    down.wait()
    table[0:8] = split_table(jnp.where(me == 0, 0.0, halo[0]))
    table[8:136] = own[...]
    table[136:144] = split_table(jnp.where(me == DEVICES - 1, 0.0, halo[1]))
    loads[5].wait()
    loads[6].wait()
    elem_blocks(table, mats, nodes, stiff, *SHARE_ROWS)
    wait_copies(got, DEVICES, sems, 4)

    loads[7].wait()
    loads[8].wait()
    sum_rows(got, left, near, row_acc, near_out, part_ref)
    for k in range(1, fems):
        remote(part_ref, parts.at[f], sems, 6, (lax.rem(f + k, fems), b)).start()
    parts[f] = part_ref[...]
    elem_blocks(table, mats, nodes, stiff, *SHARE_COUPLING)
    wait_copies(parts, fems, sems, 6)

    loads[9].wait()
    far_field(parts, right, shares)
    shares[b] = shares[b] + near_out[...]
    for k in range(1, bems):
        peer = lax.rem(b + k, bems)
        remote(shares.at[peer], sums.at[b], sems, 8, (f, peer)).start()
    sums[b] = shares[b]
    elem_blocks(table, mats, nodes, stiff, *SHARE_FLUX)
    wait_copies(sums, bems, sems, 8)

    loads[10].wait()
    flux = bem_ref[...]
    for k in range(bems):
        flux = flux + sums[k]
    flux_out[...] = flux
    flux_f32[...] = jnp.zeros_like(flux_f32)
    for t in range(9):
        flux_f32[4 * t : 4 * t + 4] = flux[:, 128 * t : 128 * t + 128]
    flux_table[...] = split_table(flux_f32[...])

    def fill_back(peers):
        pos = jnp.concatenate([got[p, 4:5] for p in peers], 1).astype(i32)
        x = pick(flux_table[...], onehot(128, to_bf(pos & 127)), pos >> 7, 5)
        for j, p in enumerate(peers):
            send_back[p] = x[0:4, 256 * j : 256 * j + 256]

    send_chunks(me, send_back, got_back, sems, 10, fill_back)
    elem_blocks(table, mats, nodes, stiff, *SHARE_BACK)
    wait_copies(got_back, DEVICES, sems, 10)

    add_returned(got_back, slots, stiff)
    for q in range(32):
        a = stiff[8 * q : 8 * q + 8]
        fem_out[:, 256 * q : 256 * q + 256] = (a + pltpu.roll(a, 4, axis=0))[0:4]


def whole_call(*args):
    vmem = pl.BlockSpec(memory_space=pltpu.VMEM)
    hbm = pl.BlockSpec(memory_space=pl.ANY)
    rows, elems = args[2].shape[1], args[8].shape[1]
    return pl.pallas_call(
        whole_kernel,
        in_specs=[pl.BlockSpec(memory_space=pltpu.SMEM)] + [hbm] * 11,
        out_specs=[vmem] * 2,
        out_shape=[jax.ShapeDtypeStruct((4, 8192), f32), jax.ShapeDtypeStruct((4, 1152), f32)],
        scratch_shapes=[
            pltpu.VMEM((4, 8192), f32),
            pltpu.VMEM((1, rows), i32),
            pltpu.VMEM((1, rows), i32),
            pltpu.VMEM((1, rows), i32),
            pltpu.VMEM((1, rows), f32),
            pltpu.VMEM((4, 1152), f32),
            pltpu.VMEM((128, 256), f32),
            pltpu.VMEM((4, 4, elems), f32),
            pltpu.VMEM((4, elems), i32),
            pltpu.VMEM((512, 1152), bf16),
            pltpu.VMEM((9, 128, 128), bf16),
            pltpu.VMEM((512, 1152), bf16),
            pltpu.VMEM((1024, 256), f32),
            pltpu.VMEM((DEVICES, 8, 256), f32),
            pltpu.VMEM((144, 512), bf16),
            pltpu.VMEM((128, 512), bf16),
            pltpu.VMEM((2, 8, 256), f32),
            pltpu.VMEM((DEVICES, 5, 256), f32),
            pltpu.VMEM((DEVICES, 5, 256), f32),
            pltpu.VMEM((80, 128), f32),
            pltpu.VMEM((4, 512), f32),
            pltpu.VMEM((4, 1152), f32),
            pltpu.VMEM((8, 4, 512), f32),
            pltpu.VMEM((16, 4, 1152), f32),
            pltpu.VMEM((16, 4, 1152), f32),
            pltpu.VMEM((40, 128), f32),
            pltpu.VMEM((40, 256), bf16),
            pltpu.VMEM((DEVICES, 4, 256), f32),
            pltpu.VMEM((DEVICES, 4, 256), f32),
            pltpu.VMEM((256, 256), f32),
            pltpu.SemaphoreType.DMA((12,)),
            pltpu.SemaphoreType.DMA((11,)),
        ],
        compiler_params=pltpu.CompilerParams(
            collective_id=0, has_side_effects=True, vmem_limit_bytes=VMEM_LIMIT
        ),
        name="whole",
    )(*args)


def per_device(
    fem_field,
    elem_mats,
    elem_nodes,
    trace_count,
    trace_node,
    trace_block,
    trace_pos,
    trace_weight,
    near_tiles,
    left_basis,
    right_basis,
    bem_field,
):
    out, flux = whole_call(
        trace_count,
        fem_field,
        trace_node.reshape(1, -1),
        trace_block.reshape(1, -1),
        trace_pos.reshape(1, -1),
        trace_weight.reshape(1, -1),
        bem_field[0],
        elem_mats,
        elem_nodes,
        left_basis.reshape(512, 1152),
        near_tiles[0],
        right_basis.reshape(512, 1152),
    )
    return out, flux[None]


def solution(mesh):
    placed = (
        P(None, ("fem", "bem")),
        P(None, None, ("fem", "bem")),
        P(None, ("fem", "bem")),
        P(("fem", "bem")),
        P(("fem", "bem")),
        P(("fem", "bem"), None),
        P(("fem", "bem")),
        P(("fem", "bem")),
        P("bem", "fem", None, None),
        P("bem", None, None, "fem"),
        P("bem", None, None, "fem"),
        P("bem", None, "fem"),
    )
    return jax.shard_map(
        per_device,
        mesh=mesh,
        in_specs=placed,
        out_specs=(P(None, ("fem", "bem")), P("bem", None, "fem")),
        check_vma=False,
    )
```

time: 2110 us -> 92 us (0.04)
  other arithmetic: 1280 us -> 0 us
  local copies, waits for them, and re-layouts: 646 us -> 2.9 us
  Pallas kernels: 0 us -> 87.1 us
  waiting for transfers between devices: 84.8 us -> 0 us
  starting transfers between devices: 32.1 us -> 0 us
  blocking collectives: 27.9 us -> 0 us
    scatter-add x3 -> x0, other arithmetic: 1090 us -> none  [the longest x1 696 us: stiffness_local(): assembled.at[:, target.reshape(-1)]]
    gather x2 -> x0, local copies, waits for them, and re-layouts: 467 us -> none  [stiffness_local(): corner = extended[:, elem_nodes]]
    scatter x1 -> x0, other arithmetic: 147 us -> none  [per_device(): jnp.zeros((rhs_count, bucket_count * capacity), jnp.float32)]
    pallas_call x0 -> x1, Pallas kernels: none -> 87.1 us  [whole_call(): pl.pallas_call(whole_kernel, in_specs=[pl.BlockSpec(memory_space=pltpu.SM...]
    unnamed x3 -> x0, waiting for transfers between devices: 75.3 us -> none
    scatter x1 -> x0, local copies, waits for them, and re-layouts: 60.4 us -> none  [per_device(): send_offsets = jnp.zeros((1, bucket_count * capacity), jnp.float32).at[:,...]
    reshape x4 -> x0, local copies, waits for them, and re-layouts: 51.3 us -> none  [the longest x1 30.9 us: stiffness_local(): contrib.reshape(rhs_count, -1)]
    all_gather x1 -> x0, local copies, waits for them, and re-layouts: 33.9 us -> none  [per_device(): whole_flux = lax.all_gather(bem_flux, ('fem', 'bem'), axis=0, tiled=True)]
  transfers between devices with their start and end apart: 8 -> 0, of which waited for: 2 -> 0; matrix products, arithmetic and copies ran while one was open for 70% -> 0% of each run, Pallas kernels for 0% -> 0%
where the time goes in v3:
time: 92 us; the launch traced here: 91.3 us
  Pallas kernels  87.1 us (95%)
  local copies, waits for them, and re-layouts  2.9 us (3%)
  between operations  1.29 us (1%)
    pallas_call x1, Pallas kernels, whole_call(): pl.pallas_call(whole_kernel, in_specs=[pl.BlockSpec(memory_space=pltpu.SM...  87.1 us
    unnamed x2, local copies, waits for them, and re-layouts  2.9 us

profile of v3, /device:TPU:1, one launch (start us, length us, event | category | flops | bytes accessed | tf_op | source)
XLA Modules:
  0.0 91.3 jit_solution(8637142790070830937)
XLA Ops:
  1.3 87.1 %whole.1 = (f32[4,8192]{1,0:T(4,128)}, f32[4,1152]{1,0:T(4,128)}) custom-call(s32[1]{0:T(128)S(6)} %copy.16.count_ref, f32[4,8192]{1,0:T(4,128)} %field_hbm.1, s32[1,16384]{1,0:T(1,128)} %bitcast.12, s32[1,16384]{1,0:T(1,128)} %bitcast.13, s32[1,16384]{1,0:T(1,128)} %bitcast.14, f32[1,16384]{1,0:T(1,128)} %bitcast.15, f32[4,1152]{1,0:T(4,128)} %bitcast.16, ...), custom_call_target="tpu_custom_call" | custom-call | tf_op jit(solution)/shard_map/whole/pallas_call | solution.py:420
  88.4 1.6 %copy.17 = f32[4,8192]{1,0:T(4,128)} copy(f32[4,8192]{1,0:T(4,128)} %get-tuple-element.8) | data formatting | bytes 262144
  90.0 1.3 %copy.18 = f32[1,4,1152]{2,1,0:T(4,128)} copy(f32[1,4,1152]{2,1,0:T(4,128)} %bitcast.17) | data formatting | bytes 36864

commit v4 on v3

--- a/solution.py
+++ b/solution.py
@@ -8,7 +8,7 @@
 from jax.sharding import PartitionSpec as P
 
 ELEM_BLOCK = 2048
-ROW_BLOCK = 2048
+ROW_BLOCK = 4096
 SHARE_ROWS = (0, 6)
 SHARE_COUPLING = (6, 2)
 SHARE_FLUX = (8, 3)
@@ -94,11 +94,17 @@
         out_ref[...] += total
 
 
-def bucket_rows(count_ref, node_ref, block_ref, pos_ref, weight_ref, out_ref, acc):
+def coded(exponent, mantissa, negative):
+    size = ((mantissa + 128) << exponent).astype(f32)
+    return jnp.where(negative, -size, size)
+
+
+def bucket_rows(count_ref, node_ref, block_ref, pos_ref, weight_ref, out_ref, acc, meanwhile):
     rb = ROW_BLOCK
     acc[...] = jnp.zeros_like(acc)
 
     def step(i, before):
+        meanwhile(i)
         at = pl.ds(pl.multiple_of(i * rb, rb), rb)
         node, pos, block = node_ref[:, at], pos_ref[:, at], block_ref[:, at]
         row = i * rb + iota((1, rb), 1)
@@ -116,26 +122,42 @@
         slot = onehot(256, jnp.concatenate(ranks, 1).astype(bf16))
 
         hi = coef.astype(bf16).astype(f32)
-        sub = iota((8, rb), 0)
-        part = jnp.zeros((8, rb), f32)
-        highs = (pos >> 7).astype(f32), (node >> 8).astype(f32), hi
-        lows = (pos & 127).astype(f32), (node & 255).astype(f32), coef - hi
-        for k in range(3):
-            part = jnp.where(sub == k, jnp.broadcast_to(highs[k], (8, rb)), part)
-            part = jnp.where(sub == k + 4, jnp.broadcast_to(lows[k], (8, rb)), part)
-        acc[...] += lax.dot_general(
-            spread(part, bucket, 64), slot, NT, preferred_element_type=f32
+        first = coded(pos >> 7, pos & 127, (node & 4096) > 0)
+        second = coded((node >> 7) & 15, node & 127, (node & 2048) > 0)
+        sub = iota((16, rb), 0) & 3
+        part = jnp.broadcast_to(coef - hi, (16, rb))
+        for k, item in enumerate((first, second, hi)):
+            part = jnp.where(sub == k, jnp.broadcast_to(item, (16, rb)), part)
+        part = part.astype(bf16)
+        at16 = to_bf(jnp.broadcast_to(bucket, (16, rb)) - (iota((16, rb), 0) >> 2))
+        zero = jnp.zeros((), bf16)
+        spread4 = jnp.concatenate(
+            [jnp.where(at16 == jnp.asarray(4 * j, bf16), part, zero) for j in range(32)], 0
         )
+        acc[...] += lax.dot_general(spread4, slot, NT, preferred_element_type=f32)
         return before
 
     lax.fori_loop(0, node_ref.shape[1] // rb, step, jnp.zeros((128, 1), f32))
 
-    @pl.loop(0, 128)
-    def _(b):
-        c = acc[pl.ds(pl.multiple_of(b * 8, 8), 8), :]
-        s = iota(c.shape, 0)
-        c = c * jnp.where(s == 0, 128.0, jnp.where(s == 1, 256.0, 1.0))
-        out_ref[b] = c + pltpu.roll(c, 4, axis=0)
+    rows = 64
+
+    @pl.loop(0, 512 // rows)
+    def _(i):
+        v = acc[pl.ds(pl.multiple_of(i * rows, rows), rows), :]
+        size = jnp.abs(v)
+        sign = jnp.where(v < 0, 1.0, 0.0)
+        e = jnp.zeros(v.shape, i32)
+        for k in range(1, 16):
+            e = e + jnp.where(size >= 128.0 * 2**k, 1, 0)
+        code = ((e << 7) + (size.astype(i32) >> e) - 128).astype(f32)
+        kind = iota(v.shape, 0) & 3
+        node = code + 2048.0 * sign + 4096.0 * pltpu.roll(sign, 1, axis=0)
+        coef = v + pltpu.roll(v, rows - 1, axis=0)
+        out = jnp.where(kind == 0, code, jnp.where(kind == 1, node, coef))
+        for j in range(rows // 8):
+            tile = out[8 * j : 8 * j + 8]
+            out_ref[i * (rows // 4) + 2 * j] = tile
+            out_ref[i * (rows // 4) + 2 * j + 1] = pltpu.roll(tile, 4, axis=0)
 
 
 DEVICES = 128
@@ -146,14 +168,11 @@
     return (index // wide, lax.rem(index, wide))
 
 
-def greet_all(me):
+def greet(me, first, count):
     barrier = pltpu.get_barrier_semaphore()
-
-    @pl.loop(1, DEVICES)
-    def _(k):
-        pl.semaphore_signal(
-            barrier, inc=1, device_id=place(lax.rem(me + k, DEVICES)), device_id_type=MESH
-        )
+    for k in range(count):
+        peer = lax.rem(me + first + k, DEVICES)
+        pl.semaphore_signal(barrier, inc=1, device_id=place(peer), device_id_type=MESH)
 
 
 def await_all():
@@ -176,7 +195,7 @@
 
 
 def send_chunks(me, send, got, sems, at, fill):
-    group = 8
+    group = 16
 
     def chunk(i, last):
         peers = [lax.rem(me + i * group + j + 1, DEVICES) for j in range(group)]
@@ -272,7 +291,7 @@
     left_hbm,
     near_hbm,
     right_hbm,
-    fem_out,
+    stiff,
     flux_out,
     field,
     node_ref,
@@ -303,7 +322,6 @@
     flux_table,
     send_back,
     got_back,
-    stiff,
     sems,
     local_sems,
 ):
@@ -328,14 +346,26 @@
     ]
     for load in loads:
         load.start()
-    greet_all(me)
+    greet(me, 1, 7)
     stiff[...] = jnp.zeros_like(stiff)
-    for load in loads[:5]:
+    for load in loads[:4]:
         load.wait()
+    steps = node_ref.shape[1] // ROW_BLOCK
+    share = (DEVICES - 8) // steps
+    bucket_rows(
+        count_ref,
+        node_ref,
+        block_ref,
+        pos_ref,
+        weight_ref,
+        slots,
+        bucket_acc,
+        lambda i: greet(me, 8 + i * share, share),
+    )
+    loads[4].wait()
     for q in range(32):
         field_ref[4 * q : 4 * q + 4] = field[:, 256 * q : 256 * q + 256]
     own[...] = split_table(field_ref[...])
-    bucket_rows(count_ref, node_ref, block_ref, pos_ref, weight_ref, slots, bucket_acc)
 
     await_all()
     up = remote(
@@ -408,9 +438,6 @@
     wait_copies(got_back, DEVICES, sems, 10)
 
     add_returned(got_back, slots, stiff)
-    for q in range(32):
-        a = stiff[8 * q : 8 * q + 8]
-        fem_out[:, 256 * q : 256 * q + 256] = (a + pltpu.roll(a, 4, axis=0))[0:4]
 
 
 def whole_call(*args):
@@ -421,7 +448,7 @@
         whole_kernel,
         in_specs=[pl.BlockSpec(memory_space=pltpu.SMEM)] + [hbm] * 11,
         out_specs=[vmem] * 2,
-        out_shape=[jax.ShapeDtypeStruct((4, 8192), f32), jax.ShapeDtypeStruct((4, 1152), f32)],
+        out_shape=[jax.ShapeDtypeStruct((256, 256), f32), jax.ShapeDtypeStruct((4, 1152), f32)],
         scratch_shapes=[
             pltpu.VMEM((4, 8192), f32),
             pltpu.VMEM((1, rows), i32),
@@ -435,7 +462,7 @@
             pltpu.VMEM((512, 1152), bf16),
             pltpu.VMEM((9, 128, 128), bf16),
             pltpu.VMEM((512, 1152), bf16),
-            pltpu.VMEM((1024, 256), f32),
+            pltpu.VMEM((512, 256), f32),
             pltpu.VMEM((DEVICES, 8, 256), f32),
             pltpu.VMEM((144, 512), bf16),
             pltpu.VMEM((128, 512), bf16),
@@ -452,7 +479,6 @@
             pltpu.VMEM((40, 256), bf16),
             pltpu.VMEM((DEVICES, 4, 256), f32),
             pltpu.VMEM((DEVICES, 4, 256), f32),
-            pltpu.VMEM((256, 256), f32),
             pltpu.SemaphoreType.DMA((12,)),
             pltpu.SemaphoreType.DMA((11,)),
         ],
@@ -461,6 +487,25 @@
         ),
         name="whole",
     )(*args)
+
+
+def finish_kernel(parts_ref, flux_ref, fem_out, flux_out):
+    flux_out[0] = flux_ref[...]
+    for q in range(32):
+        a = parts_ref[8 * q : 8 * q + 8]
+        fem_out[:, 256 * q : 256 * q + 256] = (a + pltpu.roll(a, 4, axis=0))[0:4]
+
+
+def finish_call(parts, flux):
+    vmem = pl.BlockSpec(memory_space=pltpu.VMEM)
+    return pl.pallas_call(
+        finish_kernel,
+        in_specs=[vmem] * 2,
+        out_specs=[vmem] * 2,
+        out_shape=[jax.ShapeDtypeStruct((4, 8192), f32), jax.ShapeDtypeStruct((1, 4, 1152), f32)],
+        compiler_params=pltpu.CompilerParams(vmem_limit_bytes=VMEM_LIMIT),
+        name="finish",
+    )(parts, flux)
 
 
 def per_device(
@@ -477,7 +522,7 @@
     right_basis,
     bem_field,
 ):
-    out, flux = whole_call(
+    parts, flux = whole_call(
         trace_count,
         fem_field,
         trace_node.reshape(1, -1),
@@ -491,7 +536,7 @@
         near_tiles[0],
         right_basis.reshape(512, 1152),
     )
-    return out, flux[None]
+    return finish_call(parts, flux)
 
 
 def solution(mesh):

time: 92 us -> 85.9 us (0.934)
  local copies, waits for them, and re-layouts: 2.9 us -> 0 us
  Pallas kernels: 87.1 us -> 84.5 us
    pallas_call x1, Pallas kernels: 87.1 us -> 82.9 us  [whole_call(): pl.pallas_call(whole_kernel, in_specs=[pl.BlockSpec(memory_space=pltpu.SM...]
    unnamed x2 -> x0, local copies, waits for them, and re-layouts: 2.9 us -> none
    pallas_call x0 -> x1, Pallas kernels: none -> 1.64 us  [finish_call(): pl.pallas_call(finish_kernel, in_specs=[vmem] * 2, out_specs=[vmem] * 2,...]
where the time goes in v4:
time: 85.9 us; the launch traced here: 85.8 us
  Pallas kernels  84.5 us (98%)
  between operations  1.29 us (2%)
    pallas_call x1, Pallas kernels, whole_call(): pl.pallas_call(whole_kernel, in_specs=[pl.BlockSpec(memory_space=pltpu.SM...  82.9 us

profile of v4, /device:TPU:1, one launch (start us, length us, event | category | flops | bytes accessed | tf_op | source)
XLA Modules:
  0.0 85.8 jit_solution(4477901811991075097)
XLA Ops:
  1.3 82.9 %whole.1 = (f32[256,256]{1,0:T(8,128)}, f32[4,1152]{1,0:T(4,128)}) custom-call(s32[1]{0:T(128)S(6)} %copy.14.count_ref, f32[4,8192]{1,0:T(4,128)} %field_hbm.1, s32[1,16384]{1,0:T(1,128)} %bitcast.11, s32[1,16384]{1,0:T(1,128)} %bitcast.12, s32[1,16384]{1,0:T(1,128)} %bitcast.13, f32[1,16384]{1,0:T(1,128)} %bitcast.14, f32[4,1152]{1,0:T(4,128)} %bitcast.15, ...), custom_call_target="tpu_custom_call" | custom-call | tf_op jit(solution)/shard_map/whole/pallas_call | solution.py:447
  84.2 1.6 %finish.1 = (f32[4,8192]{1,0:T(4,128)}, f32[1,4,1152]{2,1,0:T(4,128)}) custom-call(f32[256,256]{1,0:T(8,128)} %get-tuple-element.4.parts_ref, f32[4,1152]{1,0:T(4,128)} %get-tuple-element.5.flux_ref), custom_call_target="tpu_custom_call" | custom-call | tf_op jit(solution)/shard_map/finish/pallas_call | solution.py:501

commit v5 on v4

--- a/solution.py
+++ b/solution.py
@@ -7,12 +7,12 @@
 from jax.experimental.pallas import tpu as pltpu
 from jax.sharding import PartitionSpec as P
 
-ELEM_BLOCK = 2048
-ROW_BLOCK = 4096
-SHARE_ROWS = (0, 6)
-SHARE_COUPLING = (6, 2)
-SHARE_FLUX = (8, 3)
-SHARE_BACK = (11, 5)
+ELEM_BLOCK = 4096
+ROW_BLOCK = 8192
+SHARE_ROWS = (0, 3)
+SHARE_COUPLING = (3, 1)
+SHARE_FLUX = (4, 2)
+SHARE_BACK = (6, 2)
 bf16 = jnp.bfloat16
 f32 = jnp.float32
 i32 = jnp.int32
@@ -219,7 +219,7 @@
 
 def sum_rows(got, left, near, acc, near_out, part_ref):
     acc[...] = jnp.zeros_like(acc)
-    group = 16
+    group = 32
 
     @pl.loop(0, DEVICES // group)
     def _(i):
@@ -261,7 +261,7 @@
 
 
 def add_returned(got, slots, acc):
-    group = 16
+    group = 32
 
     @pl.loop(0, DEVICES // group)
     def _(i):

time: 85.9 us -> 82 us (0.955)
  Pallas kernels: 84.5 us -> 80.6 us
    pallas_call x1, Pallas kernels: 82.9 us -> 79 us  [whole_call(): pl.pallas_call(whole_kernel, in_specs=[pl.BlockSpec(memory_space=pltpu.SM...]
where the time goes in v5:
time: 82 us; the launch traced here: 81.9 us
  Pallas kernels  80.6 us (98%)
  between operations  1.29 us (2%)
    pallas_call x1, Pallas kernels, whole_call(): pl.pallas_call(whole_kernel, in_specs=[pl.BlockSpec(memory_space=pltpu.SM...  79 us

profile of v5, /device:TPU:1, one launch (start us, length us, event | category | flops | bytes accessed | tf_op | source)
XLA Modules:
  0.0 81.9 jit_solution(10355230543187090130)
XLA Ops:
  1.3 79.0 %whole.1 = (f32[256,256]{1,0:T(8,128)}, f32[4,1152]{1,0:T(4,128)}) custom-call(s32[1]{0:T(128)S(6)} %copy.14.count_ref, f32[4,8192]{1,0:T(4,128)} %field_hbm.1, s32[1,16384]{1,0:T(1,128)} %bitcast.11, s32[1,16384]{1,0:T(1,128)} %bitcast.12, s32[1,16384]{1,0:T(1,128)} %bitcast.13, f32[1,16384]{1,0:T(1,128)} %bitcast.14, f32[4,1152]{1,0:T(4,128)} %bitcast.15, ...), custom_call_target="tpu_custom_call" | custom-call | tf_op jit(solution)/shard_map/whole/pallas_call | solution.py:447
  80.3 1.6 %finish.1 = (f32[4,8192]{1,0:T(4,128)}, f32[1,4,1152]{2,1,0:T(4,128)}) custom-call(f32[256,256]{1,0:T(8,128)} %get-tuple-element.4.parts_ref, f32[4,1152]{1,0:T(4,128)} %get-tuple-element.5.flux_ref), custom_call_target="tpu_custom_call" | custom-call | tf_op jit(solution)/shard_map/finish/pallas_call | solution.py:501

commit v6 on v5

--- a/solution.py
+++ b/solution.py
@@ -195,7 +195,7 @@
 
 
 def send_chunks(me, send, got, sems, at, fill):
-    group = 16
+    group = 32
 
     def chunk(i, last):
         peers = [lax.rem(me + i * group + j + 1, DEVICES) for j in range(group)]

time: 82 us -> 81 us (0.988)
  Pallas kernels: 80.6 us -> 79.5 us
    pallas_call x1, Pallas kernels: 79 us -> 77.9 us  [whole_call(): pl.pallas_call(whole_kernel, in_specs=[pl.BlockSpec(memory_space=pltpu.SM...]
where the time goes in v6:
time: 81 us; the launch traced here: 80.8 us
  Pallas kernels  79.5 us (98%)
  between operations  1.29 us (2%)
    pallas_call x1, Pallas kernels, whole_call(): pl.pallas_call(whole_kernel, in_specs=[pl.BlockSpec(memory_space=pltpu.SM...  77.9 us
    pallas_call x1, Pallas kernels, finish_call(): pl.pallas_call(finish_kernel, in_specs=[vmem] * 2, out_specs=[vmem] * 2,...  1.64 us

profile of v6, /device:TPU:1, one launch (start us, length us, event | category | flops | bytes accessed | tf_op | source)
XLA Modules:
  0.0 80.8 jit_solution(10538898955943918793)
XLA Ops:
  1.3 77.9 %whole.1 = (f32[256,256]{1,0:T(8,128)}, f32[4,1152]{1,0:T(4,128)}) custom-call(s32[1]{0:T(128)S(6)} %copy.14.count_ref, f32[4,8192]{1,0:T(4,128)} %field_hbm.1, s32[1,16384]{1,0:T(1,128)} %bitcast.11, s32[1,16384]{1,0:T(1,128)} %bitcast.12, s32[1,16384]{1,0:T(1,128)} %bitcast.13, f32[1,16384]{1,0:T(1,128)} %bitcast.14, f32[4,1152]{1,0:T(4,128)} %bitcast.15, ...), custom_call_target="tpu_custom_call" | custom-call | tf_op jit(solution)/shard_map/whole/pallas_call | solution.py:447
  79.2 1.6 %finish.1 = (f32[4,8192]{1,0:T(4,128)}, f32[1,4,1152]{2,1,0:T(4,128)}) custom-call(f32[256,256]{1,0:T(8,128)} %get-tuple-element.4.parts_ref, f32[4,1152]{1,0:T(4,128)} %get-tuple-element.5.flux_ref), custom_call_target="tpu_custom_call" | custom-call | tf_op jit(solution)/shard_map/finish/pallas_call | solution.py:501
